TPU v7x, 32 devices: a whole 2x2x4 slice. The times are simulated.
32 devices in a mesh: wide: 8 (over y, x, core), narrow: 4 (over z).
Axes of the slice: x: 2, y: 2, z: 4, core: 2. Of those that a mesh axis runs over, the one named last changes fastest.
Arguments:
- hamiltonian_tiles: float32 [12288, 6144], P('wide', 'narrow'), may hold values from -0.0546875 to 0.0546875
- row_columns: int32 [8, 4], P('wide'), may hold values from 0 to 7, as said below
- start_vectors: float32 [12288, 128], P(('wide', 'narrow')), may hold values from -60 to 60
Outputs:
- new_vectors: float32 [12288, 128], P(('wide', 'narrow'))
Inputs may be any that keep to these rules, and one draw needn't show every extreme that they name: For block row r = w + j // 4, row_columns[w, j] = (r + d) mod 8, with d = 0 where j % 4 = 0 and, for the other tiles of that block row, distinct d between 1 and 7; a block's mirror may also be stored.
All inputs are finite; a program needn't handle non-finite values.
Results may differ from a plain program's by a relative error of at most 0.0003.
Values sent between devices are 32-bit elements; how exact they have to be, the bound alone decides.
A program may use at most 64 MiB of HBM per device.

v0:
```python
import functools

import jax
import jax.numpy as jnp
from jax import lax
from jax.experimental import pallas as pl
from jax.experimental.pallas import tpu as pltpu
from jax.sharding import PartitionSpec as P

ITERS = 2
NS_STEPS = 5
HIGHEST = lax.Precision.HIGHEST


def flip(x, mask):
    bit = 1
    while bit <= mask:
        if mask & bit:
            x = x + bit * (1 - 2 * ((x // bit) % 2))
        bit *= 2
    return x


def bits_of(count):
    bits = count.bit_length() - 1
    assert count == 1 << bits
    return bits


def orders(wide):
    bits = list(range(1, bits_of(wide)))
    return bits + [0], bits[::-1] + [0]


def position(relative, order):
    return sum(((relative >> bit) & 1) << place for place, bit in enumerate(order))


def inverse_root(gram, total):
    size = gram.shape[0]
    row = lax.broadcasted_iota(jnp.int32, (size, size), 0)
    column = lax.broadcasted_iota(jnp.int32, (size, size), 1)
    identity = jnp.where(row == column, 1.0, 0.0).astype(jnp.float32)
    square = jnp.sum(gram * gram, axis=1, keepdims=True)
    scale = jnp.sqrt(jnp.sum(square, axis=0, keepdims=True) + 1e-06)
    current = gram / scale
    inverse = identity
    for repeat in range(NS_STEPS):
        if repeat == 0:
            middle = 1.5 * identity - 0.5 * current
        else:
            middle = 1.5 * identity - 0.5 * jnp.dot(inverse, current, precision=HIGHEST)
        if repeat < NS_STEPS - 1:
            current = jnp.dot(current, middle, precision=HIGHEST)
        inverse = middle if repeat == 0 else jnp.dot(middle, inverse, precision=HIGHEST)
    return inverse * jnp.sqrt(total / scale)


def split(x):
    high = x.astype(jnp.bfloat16)
    low = (x - high.astype(jnp.float32)).astype(jnp.bfloat16)
    return high, low


def kernel(wide, narrow, out_cuts, places, tile_hbm, start, out, stage, tile_hi, tile_lo, block, columns,
           left, right, trans, direct, own, high, rowp, gath, pick, picked, tpart, dpart,
           placed, came, merged, last, grams, stage_sem, send_sem, recv_sem):
    me_w = lax.axis_index("wide")
    me_z = lax.axis_index("narrow")
    order = trans.shape[0]
    rows, width = own.shape[1], own.shape[2]
    halves = narrow // 2
    wbits = bits_of(wide)
    hbits = bits_of(halves)
    two_orders = orders(wide)
    mate = flip(me_z, 1)
    wide_peers = [{"wide": flip(me_w, 1 << bit), "narrow": me_z} for bit in range(wbits)]
    near_peers = [
        {"wide": me_w, "narrow": flip(me_z, 1 << bit)} for bit in range(bits_of(narrow))
    ]

    barrier = pltpu.get_barrier_semaphore()
    for peer in wide_peers + near_peers:
        pl.semaphore_signal(
            barrier, inc=1, device_id=peer, device_id_type=pl.DeviceIdType.MESH
        )

    stage_rows = stage.shape[1]
    chunks = order // stage_rows

    def fetch(chunk):
        return pltpu.make_async_copy(
            tile_hbm.at[pl.ds(chunk * stage_rows, stage_rows)],
            stage.at[chunk % 2],
            stage_sem.at[chunk % 2],
        )

    fetch(0).start()
    if chunks > 1:
        fetch(1).start()
    pl.semaphore_wait(barrier, len(wide_peers) + len(near_peers))

    sent = []

    def send(source, target, peer):
        index = len(sent)
        copy = pltpu.make_async_remote_copy(
            src_ref=source,
            dst_ref=target,
            send_sem=send_sem.at[index],
            recv_sem=recv_sem.at[index],
            device_id=peer,
            device_id_type=pl.DeviceIdType.MESH,
        )
        copy.start()
        sent.append([copy, False])
        return len(sent) - 1

    def received(index):
        sent[index][0].wait_recv()

    def gone(index):
        if not sent[index][1]:
            sent[index][0].wait_send()
            sent[index][1] = True

    def natural(q):
        return pl.multiple_of(flip(me_z, q) * rows, rows)

    def load_chunk(chunk):
        fetch(chunk).wait()
        hi, lo = split(stage[chunk % 2])
        tile_hi[pl.ds(chunk * stage_rows, stage_rows), :] = hi
        tile_lo[pl.ds(chunk * stage_rows, stage_rows), :] = lo
        if chunk + 2 < chunks:
            fetch(chunk + 2).start()

    gram_peers = wide_peers + near_peers
    gram_state = {}

    def gram_begin(which, value):
        grams[which, 0] = value
        gram_state[which] = (0, send(grams.at[which, 0], grams.at[which, 1], gram_peers[0]))

    def gram_step(which):
        step, index = gram_state[which]
        received(index)
        total = grams[which, 2 * step] + grams[which, 2 * step + 1]
        step += 1
        if step == len(gram_peers):
            gram_state[which] = (step, None)
            return total
        grams[which, 2 * step] = total
        gram_state[which] = (
            step, send(grams.at[which, 2 * step], grams.at[which, 2 * step + 1], gram_peers[step])
        )
        return None

    total_rows = float(wide * order)
    step_of_columns = 256
    cuts = out_cuts
    piece = rows // cuts
    part = piece // 2
    units = [(r, c) for r in range(halves) for c in range(cuts)]
    back_units = [(r, c) for r in range(halves - 1, -1, -1) for c in range(cuts)]
    placed_sends = []
    total = None
    loaded = 0

    def whole_piece(c):
        return pl.ds(c * piece, piece)

    def side_rows(side):
        return pl.ds(side * part, part)

    for it in range(ITERS):
        far = {}
        row_in = {}
        pick_in = {}
        gathers = {}
        t_out = {}
        d_out = {}
        sums = {}
        ends = {}

        high[it, 0] = start[...] if it == 0 else own[it]
        source = start if it == 0 else high.at[it, 0]
        if halves > 1:
            for c in range(cuts):
                far[0, c] = send(
                    source.at[whole_piece(c)], high.at[it, 1, whole_piece(c)], near_peers[1]
                )

        def ready(r, c):
            if r == 0:
                return
            step = r.bit_length() - 1
            if r == 1 << step:
                received(far[step, c])
                if step + 1 < hbits:
                    count = 1 << (step + 1)
                    far[step + 1, c] = send(
                        high.at[it, pl.ds(0, count), whole_piece(c)],
                        high.at[it, pl.ds(count, count), whole_piece(c)],
                        near_peers[step + 2],
                    )

        def begin(r, c):
            base = source if r == 0 else high.at[it, r]
            for side in (2 * c, 2 * c + 1):
                gathers[r, side, 0] = send(
                    base.at[side_rows(side)],
                    gath.at[it, side, r, 1],
                    wide_peers[two_orders[side % 2][0]],
                )
            row_in[r, c] = send(
                base.at[whole_piece(c)], rowp.at[it, r, whole_piece(c)], near_peers[0]
            )
            for side in (2 * c, 2 * c + 1):
                gath[it, side, r, 0] = high[it, r, side_rows(side), :]

        def advance(r, c, step):
            for side in (2 * c, 2 * c + 1):
                received(gathers[r, side, step - 1])
                if step < wbits:
                    count = 1 << step
                    gathers[r, side, step] = send(
                        gath.at[it, side, r, pl.ds(0, count)],
                        gath.at[it, side, r, pl.ds(count, count)],
                        wide_peers[two_orders[side % 2][step]],
                    )

        def chosen(r, side, column):
            value = gath[it, side, r, 0]
            for p in range(1, wide):
                value = jnp.where(places[side % 2, column] == p, gath[it, side, r, p], value)
            return value

        def choose(r, c):
            for side in (2 * c, 2 * c + 1):
                pick[it, r, side_rows(side), :] = chosen(r, side, mate)
            pick_in[r, c] = send(
                pick.at[it, r, whole_piece(c)], picked.at[it, r, whole_piece(c)], near_peers[0]
            )
            for side in (2 * c, 2 * c + 1):
                columns[pl.ds(natural(2 * r) + side * part, part), :] = chosen(r, side, me_z)

        def transposed_terms():
            for r, c in units:
                received(row_in[r, c])
            for r in range(halves):
                block[pl.ds(natural(2 * r), rows), :] = high[it, r]
                block[pl.ds(natural(2 * r + 1), rows), :] = rowp[it, r]
            hi, lo = split(block[...].T)
            left[pl.ds(0, width), :] = hi
            left[pl.ds(width, width), :] = lo

            def body(chunk, carry):
                at = pl.multiple_of(chunk * step_of_columns, step_of_columns)
                both = jnp.dot(
                    left[...], tile_hi[:, pl.ds(at, step_of_columns)],
                    preferred_element_type=jnp.float32,
                )
                rest = jnp.dot(
                    left[pl.ds(0, width), :], tile_lo[:, pl.ds(at, step_of_columns)],
                    preferred_element_type=jnp.float32,
                )
                trans[pl.ds(at, step_of_columns), :] = (both[:width] + (both[width:] + rest)).T
                return carry

            lax.fori_loop(0, order // step_of_columns, body, 0)

        def direct_rows(q):
            at = natural(q)
            both = jnp.dot(
                tile_hi[pl.ds(at, rows), :], right[...], preferred_element_type=jnp.float32
            )
            rest = jnp.dot(
                tile_lo[pl.ds(at, rows), :], right[:, pl.ds(0, width)],
                preferred_element_type=jnp.float32,
            )
            direct[pl.ds(at, rows), :] = both[:, :width] + (both[:, width:] + rest)

        def send_rows(results, landing, group, r):
            for c in range(cuts):
                group[r, c] = send(
                    results.at[pl.ds(natural(2 * r + 1) + c * piece, piece)],
                    landing.at[it, r, whole_piece(c)],
                    near_peers[0],
                )

        def step_gram():
            return gram_step(it - 1) if it > 0 and gram_state[it - 1][1] is not None else None

        for time in range(len(units) + wbits):
            for place in range(len(units)):
                r, c = units[place]
                step = time - place
                if step == 0:
                    ready(r, c)
                    begin(r, c)
                elif 0 < step <= wbits:
                    advance(r, c, step)
                    if step == wbits:
                        choose(r, c)
            if it == 0 and loaded < chunks:
                load_chunk(loaded)
                loaded += 1
            if time % 2 == 1:
                found = step_gram()
                total = found if found is not None else total
        while loaded < chunks:
            load_chunk(loaded)
            loaded += 1

        transposed_terms()
        send_rows(trans, tpart, t_out, halves - 1)
        for r, c in units:
            received(pick_in[r, c])
        for r in range(halves):
            columns[pl.ds(natural(2 * r + 1), rows), :] = picked[it, r]
        hi, lo = split(columns[...])
        right[:, pl.ds(0, width)] = hi
        right[:, pl.ds(width, width)] = lo
        for r in range(halves - 1, -1, -1):
            direct_rows(2 * r + 1)
            send_rows(direct, dpart, d_out, r)
            if r > 0:
                send_rows(trans, tpart, t_out, r - 1)
        for r in range(halves - 1, -1, -1):
            direct_rows(2 * r)

        for index in placed_sends:
            gone(index)
        placed_sends = []

        def put(r, side, first, count):
            mine = trans[pl.ds(natural(2 * r) + side * part, part), :]
            other = tpart[it, r, side_rows(side), :]
            for p in range(first, first + count):
                placed[side, r, p] = jnp.where(
                    places[side % 2, me_z] == p, mine, 0.0
                ) + jnp.where(places[side % 2, mate] == p, other, 0.0)

        def pass_on(r, side, step):
            count = 1 << step
            index = send(
                placed.at[side, r, pl.ds(count, count)],
                came.at[it, side, r, pl.ds(count, count)],
                wide_peers[two_orders[side % 2][step]],
            )
            sums[r, side, step] = index
            placed_sends.append(index)

        def merge(r, c):
            received(d_out[r, c])
            for side in (2 * c, 2 * c + 1):
                at = side_rows(side)
                merged[it, r, at, :] = (
                    placed[side, r, 0]
                    + direct[pl.ds(natural(2 * r) + side * part, part), :]
                    + dpart[it, r, at, :]
                )
            if r >= max(1, halves // 2):
                ends[r, c] = send(
                    merged.at[it, r, whole_piece(c)],
                    last.at[it, r, whole_piece(c)],
                    near_peers[hbits],
                )

        for time in range(len(back_units) + wbits):
            for place in range(len(back_units)):
                r, c = back_units[place]
                step = wbits - 1 - (time - place)
                sides = (2 * c, 2 * c + 1)
                if step == wbits - 1:
                    received(t_out[r, c])
                    for side in sides:
                        put(r, side, wide // 2, wide // 2)
                        pass_on(r, side, step)
                    for side in sides:
                        put(r, side, 0, wide // 2)
                elif -1 <= step < wbits - 1:
                    count = 1 << (step + 1)
                    for side in sides:
                        received(sums[r, side, step + 1])
                        for p in range(count - 1, -1, -1):
                            placed[side, r, p] = placed[side, r, p] + came[it, side, r, count + p]
                        if step >= 0:
                            pass_on(r, side, step)
                    if step < 0:
                        merge(r, c)
            if time % 2 == 1:
                found = step_gram()
                total = found if found is not None else total
        if it > 0:
            while gram_state[it - 1][1] is not None:
                total = gram_step(it - 1)
            grams[0, 2 * len(gram_peers)] = inverse_root(total, total_rows)

        for r, c in ends:
            received(ends[r, c])
            merged[it, r - halves // 2, whole_piece(c), :] = (
                merged[it, r - halves // 2, whole_piece(c), :] + last[it, r, whole_piece(c), :]
            )
        for bit in range(hbits - 2, -1, -1):
            count = 1 << bit
            received(send(
                merged.at[it, pl.ds(count, count)],
                last.at[it, pl.ds(count, count)],
                near_peers[bit + 1],
            ))
            for r in range(count):
                merged[it, r] = merged[it, r] + last[it, count + r]
        for index in list(t_out.values()) + list(d_out.values()):
            gone(index)
        product = merged[it, 0]
        own[it + 1] = product
        gram_now = jnp.dot(product.T, product, precision=HIGHEST)
        gram_begin(it, gram_now)

    root = grams[0, 2 * len(gram_peers)]
    total = None
    while total is None:
        total = gram_step(1)
    gram = jnp.dot(root.T, jnp.dot(total, root, precision=HIGHEST), precision=HIGHEST)
    root = jnp.dot(root, inverse_root(gram, total_rows), precision=HIGHEST)
    out[...] = jnp.dot(own[ITERS], root, precision=HIGHEST)
    for index in range(len(sent)):
        gone(index)


def on_device(hamiltonian_tiles, row_columns, start_vectors):
    wide, narrow = lax.axis_size("wide"), lax.axis_size("narrow")
    order = hamiltonian_tiles.shape[0]
    rows, width = start_vectors.shape
    assert rows * narrow == order
    halves = narrow // 2
    wbits, nbits = bits_of(wide), bits_of(narrow)
    relative = jnp.bitwise_xor(row_columns[0], lax.axis_index("wide").astype(jnp.int32))
    places = jnp.stack([position(relative, order_) for order_ in orders(wide)])
    cuts = 2 if halves <= 2 else 1
    copies = ITERS * (
        2 * cuts * nbits + (4 * wbits + 5) * halves * cuts
    ) + ITERS * (wbits + nbits)
    f32, bf16 = jnp.float32, jnp.bfloat16
    stage_rows = order // 6
    return pl.pallas_call(
        functools.partial(kernel, wide, narrow, cuts),
        out_shape=jax.ShapeDtypeStruct((rows, width), f32),
        in_specs=[
            pl.BlockSpec(memory_space=pltpu.SMEM),
            pl.BlockSpec(memory_space=pl.ANY),
            pl.BlockSpec(memory_space=pltpu.VMEM),
        ],
        out_specs=pl.BlockSpec(memory_space=pltpu.VMEM),
        scratch_shapes=[
            pltpu.VMEM((2, stage_rows, order), f32),
            pltpu.VMEM((order, order), bf16),
            pltpu.VMEM((order, order), bf16),
            pltpu.VMEM((order, width), f32),
            pltpu.VMEM((order, width), f32),
            pltpu.VMEM((2 * width, order), bf16),
            pltpu.VMEM((order, 2 * width), bf16),
            pltpu.VMEM((order, width), f32),
            pltpu.VMEM((order, width), f32),
            pltpu.VMEM((ITERS + 1, rows, width), f32),
            pltpu.VMEM((ITERS, halves, rows, width), f32),
            pltpu.VMEM((ITERS, halves, rows, width), f32),
            pltpu.VMEM((ITERS, 2 * cuts, halves, wide, rows // (2 * cuts), width), f32),
            pltpu.VMEM((ITERS, halves, rows, width), f32),
            pltpu.VMEM((ITERS, halves, rows, width), f32),
            pltpu.VMEM((ITERS, halves, rows, width), f32),
            pltpu.VMEM((ITERS, halves, rows, width), f32),
            pltpu.VMEM((2 * cuts, halves, wide, rows // (2 * cuts), width), f32),
            pltpu.VMEM((ITERS, 2 * cuts, halves, wide, rows // (2 * cuts), width), f32),
            pltpu.VMEM((ITERS, halves, rows, width), f32),
            pltpu.VMEM((ITERS, halves, rows, width), f32),
            pltpu.VMEM((ITERS, 2 * (wbits + nbits) + 1, width, width), f32),
            pltpu.SemaphoreType.DMA((2,)),
            pltpu.SemaphoreType.DMA((copies,)),
            pltpu.SemaphoreType.DMA((copies,)),
        ],
        compiler_params=pltpu.CompilerParams(
            collective_id=0, has_side_effects=True, vmem_limit_bytes=67043328
        ),
    )(places, hamiltonian_tiles, start_vectors)


def solution(mesh):
    return jax.shard_map(
        on_device,
        mesh=mesh,
        in_specs=(P("wide", "narrow"), P("wide", None), P(("wide", "narrow"), None)),
        out_specs=P(("wide", "narrow"), None),
        check_vma=False,
    )
```

profile of v0, /device:TPU:0, one launch (start us, length us, event | category | flops | bytes accessed | tf_op | source)
XLA Modules:
  0.0 141.2 jit_solution(8184143604849942457)
XLA Ops:
  0.0 0.7 add_add_fusion.1
  0.7 0.6 pad_add_fusion.places
  1.2 138.3 %shard_map.37 = f32[384,128]{1,0:T(8,128)} custom-call(s32[2,4]{1,0:T(2,128)} %pad_add_fusion.places, f32[1536,1536]{1,0:T(8,128)} %tile_hbm.1, f32[384,128]{1,0:T(8,128)} %start.1), custom_call_target="tpu_custom_call" | custom-call | tf_op jit(solution)/shard_map/pallas_call | solution.py:448
  139.6 1.6 %copy.5 = f32[384,128]{1,0:T(8,128)} copy(f32[384,128]{1,0:T(8,128)} %shard_map.37) | data formatting | bytes 393216
where the time goes:
time: 142 us; the launch traced here: 141 us
  Pallas kernels  138 us (97%)
  local copies, waits for them, and re-layouts  1.62 us (1%)
    pallas_call x1, Pallas kernels, on_device(): pl.pallas_call(functools.partial(kernel, wide, narrow, cuts), out_shape=j...  138 us

commit v1 on v0

v1 whole, which is shorter than its diff:
```python
import functools

import jax
import jax.numpy as jnp
from jax import lax
from jax.experimental import pallas as pl
from jax.experimental.pallas import tpu as pltpu
from jax.sharding import PartitionSpec as P

ITERS = 2
NS_STEPS = 5
HIGHEST = lax.Precision.HIGHEST
MESH = pl.DeviceIdType.MESH
LOAD_CHUNKS = 6
ORDER = (
    7, 8, 9, 0, 6, 23, 15, 1, 134, 11, 24, 16, 25, 2, 17, 3, 35, 27, 28, 22, 14, 44, 43, 36,
    19, 4, 12, 5, 39, 20, 26, 10, 13, 21, 18, 55, 57, 59, 29, 31, 56, 50, 51, 52, 67, 54, 53, 40,
    32, 60, 62, 61, 45, 30, 34, 37, 65, 42, 48, 46, 38, 66, 33, 68, 47, 87, 41, 69, 75, 86, 63, 49,
    89, 95, 90, 103, 91, 94, 105, 77, 102, 70, 76, 74, 88, 107, 58, 99, 71, 80, 64, 72, 73, 81, 78, 79,
    82, 115, 93, 106, 117, 104, 114, 84, 122, 83, 97, 109, 98, 119, 116, 111, 92, 118, 96, 108, 123, 101, 100, 121,
    124, 120, 110, 125, 85, 127, 113, 112, 136, 126, 135, 129, 138, 128, 137, 130, 152, 144, 132, 151, 143, 131, 154, 153,
    133, 156, 172, 146, 163, 164, 243, 145, 155, 167, 148, 141, 168, 166, 165, 147, 196, 171, 170, 139, 140, 158, 198, 150,
    244, 149, 142, 179, 183, 180, 169, 157, 181, 182, 159, 160, 189, 191, 184, 185, 174, 162, 161, 190, 175, 176, 194, 218,
    215, 178, 177, 195, 173, 188, 217, 200, 234, 216, 193, 231, 192, 219, 199, 201, 223, 187, 203, 208, 233, 197, 186, 202,
    245, 209, 210, 227, 207, 204, 235, 205, 206, 211, 251, 226, 224, 254, 222, 232, 220, 213, 259, 238, 228, 221, 225, 253,
    212, 255, 236, 237, 239, 252, 229, 258, 230, 261, 240, 246, 247, 257, 260, 248, 249, 250, 256, 241, 262, 214, 263, 267,
    242, 265, 269, 264, 268, 266, 270, 271, 272, 273, 274, 275, 276, 277, 278,
)


def flip(x, mask):
    bit = 1
    while bit <= mask:
        if mask & bit:
            x = x + bit * (1 - 2 * ((x // bit) % 2))
        bit *= 2
    return x


def bits_of(count):
    bits = count.bit_length() - 1
    assert count == 1 << bits
    return bits


def lowest(q, bits):
    return bits if q == 0 else (q & -q).bit_length() - 1


def position(relative, order):
    return sum(((relative >> bit) & 1) << place for place, bit in enumerate(order))


class Routes:
    def __init__(self, wide, narrow):
        self.wide, self.narrow = wide, narrow
        self.wbits, self.nbits = bits_of(wide), bits_of(narrow)
        self.cuts = max(1, 4 * 4 // narrow)
        upper = list(range(1, self.wbits))
        self.lines = [upper, upper[::-1]]
        self.whole = []
        self.half = []
        for q in range(narrow):
            for c in range(self.cuts):
                if self.paired(q, c):
                    if q % 2 == 0:
                        self.whole.append((q, c))
                else:
                    self.half.append((q, c))

    def side(self, q, c):
        return (q + c) % 2

    def paired(self, q, c):
        return q < 2

    def order(self, q, c):
        line = self.lines[self.side(q, c)]
        return line + [0] if self.paired(q, c) else line[:-1] + [0]

    def last(self, q, c):
        return self.lines[self.side(q, c)][-1]

    def children(self, q):
        return [q | (1 << b) for b in range(lowest(q, self.nbits) - 1, -1, -1)]


def steps_of(routes):
    quarters, cuts = range(routes.narrow), range(routes.cuts)
    steps = [("load", i) for i in range(LOAD_CHUNKS)]
    for it in range(ITERS):
        if it > 0:
            steps.append(("turn", it))
        for q in quarters:
            for c in cuts:
                steps.append(("have", it, q, c))
        for level in range(1, routes.wbits):
            for q in quarters:
                for c in cuts:
                    paired = routes.paired(q, c)
                    if paired and q % 2 == 1:
                        continue
                    if level < len(routes.order(q, c)):
                        steps.append(("step", it, q, c, level))
        for q in quarters:
            for c in cuts:
                if not (routes.paired(q, c) and q % 2 == 1):
                    steps.append(("pick", it, q, c))
        for q in quarters[::-1]:
            steps.append(("trans", it, q))
            for c in cuts:
                if not (routes.paired(q, c) and q % 2 == 0):
                    steps.append(("pass", it, q, c))
        for q in quarters:
            for c in cuts:
                steps.append(("column", it, q, c))
        for q in quarters[::-1]:
            steps.append(("direct", it, q))
        for q in quarters[::-1]:
            for c in cuts:
                if not (routes.paired(q, c) and q % 2 == 1):
                    steps.append(("put", it, q, c))
        for level in range(routes.wbits - 1, 0, -1):
            for q in quarters[::-1]:
                for c in cuts:
                    if routes.paired(q, c) and q % 2 == 1:
                        continue
                    if level < len(routes.order(q, c)):
                        steps.append(("down", it, q, c, level))
        if it > 0:
            steps.append(("spread", it - 1))
            steps.append(("sum", it - 1))
            steps.append(("all", it - 1))
            steps += [("root", it - 1, repeat) for repeat in range(NS_STEPS)]
        for q in quarters[::-1]:
            for c in cuts:
                steps.append(("merge", it, q, c))
        for c in cuts:
            steps.append(("gram", it, c))
    steps.append(("spread", ITERS - 1))
    steps.append(("sum", ITERS - 1))
    steps.append(("all", ITERS - 1))
    steps += [("root", ITERS - 1, repeat) for repeat in range(NS_STEPS)]
    return steps


def sends_of(routes):
    count = 2
    pieces = routes.narrow * routes.cuts
    for it in range(ITERS):
        count += 2 * (routes.narrow - 1) * routes.cuts
        count += 2 * len(routes.whole) * (routes.wbits + 1)
        count += 2 * len(routes.half) * routes.wbits
        count += 2 * (routes.wide - 1) + routes.narrow - 1
    return count


def split(x):
    high = x.astype(jnp.bfloat16)
    low = (x - high.astype(jnp.float32)).astype(jnp.bfloat16)
    return high, low


def tree_sum(values):
    while len(values) > 1:
        values = [a + b for a, b in zip(values[::2], values[1::2])]
    return values[0]


def kernel(routes, sequence, slots, row_columns, tile_hbm, start, out, stage, tile_hi, tile_lo, turn_hi, turn_lo,
           rows_right, columns_right, trans, direct, whole_in, half_in, mate_rows, picks, picked, choices, chosen,
           whole_put, half_put, whole_back, half_back, passed, passed_mate, part, part_in, product, want, wants,
           grams, gram_in, gram_sum, gram_near, gram_part, gram_all, ns, roots,
           stage_sem, send_sem, recv_sem, fence_sem):
    wide, narrow, cuts = routes.wide, routes.narrow, routes.cuts
    me_w = lax.axis_index("wide")
    me_z = lax.axis_index("narrow")
    order = tile_hi.shape[0]
    rows, width = start.shape
    n = rows // cuts
    wbits = routes.wbits
    f32 = jnp.float32
    slice_rows = width // wide
    total_rows = float(wide * order)
    whole_at = {unit: place for place, unit in enumerate(routes.whole)}
    half_at = {unit: place for place, unit in enumerate(routes.half)}

    def wide_peer(mask):
        return {"wide": flip(me_w, mask), "narrow": me_z}

    def near_peer(mask):
        return {"wide": me_w, "narrow": flip(me_z, mask)}

    peers = [wide_peer(m) for m in range(1, wide)] + [near_peer(m) for m in range(1, narrow)]
    barrier = pltpu.get_barrier_semaphore()
    for peer in peers:
        pl.semaphore_signal(barrier, inc=1, device_id=peer, device_id_type=MESH)

    stage_rows = stage.shape[1]
    stages = stage.shape[0]

    def fetch(chunk):
        return pltpu.make_async_copy(
            tile_hbm.at[pl.ds(chunk * stage_rows, stage_rows)],
            stage.at[chunk % stages],
            stage_sem.at[chunk % stages],
        )

    for chunk in range(stages):
        fetch(chunk).start()

    mate = flip(me_z, 1)
    own_want = row_columns[0, me_z] ^ me_w
    mate_want = row_columns[0, mate] ^ me_w
    want[...] = jnp.full(want.shape, own_want, jnp.int32)
    pl.semaphore_wait(barrier, len(peers))

    sent = {}
    waited = set()

    def send(name, source, target, peer):
        index = len(sent)
        copy = pltpu.make_async_remote_copy(
            src_ref=source, dst_ref=target, send_sem=send_sem.at[index], recv_sem=recv_sem.at[index],
            device_id=peer, device_id_type=MESH,
        )
        copy.start()
        assert name not in sent
        sent[name] = copy

    def received(name):
        sent[name].wait_recv()

    def all_gone():
        for name, copy in sent.items():
            if name not in waited:
                copy.wait_send()
                waited.add(name)

    for side in range(2):
        send(("want", side), want, wants.at[side], wide_peer(1 << routes.lines[side][-1]))
    wants_here = set()

    def natural(q):
        return pl.multiple_of(flip(me_z, q) * rows, rows)

    def piece_at(q, c):
        return pl.ds(pl.multiple_of(natural(q) + c * n, n), n)

    def here(it):
        return it % slots

    def gathered(it, q, c):
        if routes.paired(q, c):
            return whole_in.at[here(it), whole_at[q, c]]
        return half_in.at[here(it), half_at[q, c]]

    def row_ref(it, q, c):
        if routes.paired(q, c) and q % 2 == 1:
            return mate_rows.at[here(it), whole_at[q - 1, c]]
        return gathered(it, q, c).at[0]

    def put_ref(it, q, c):
        if routes.paired(q, c):
            return whole_put.at[here(it), whole_at[q, c]]
        return half_put.at[here(it), half_at[q, c]]

    def back_ref(it, q, c):
        if routes.paired(q, c):
            return whole_back.at[here(it), whole_at[q, c]]
        return half_back.at[here(it), half_at[q, c]]

    def keep_split(target, at, value):
        hi, lo = split(value)
        target[at, pl.ds(0, width)] = hi
        target[at, pl.ds(width, width)] = lo

    def far_codes(q, c):
        side = routes.side(q, c)
        if side not in wants_here:
            received(("want", side))
            wants_here.add(side)
        code = wants[side, pl.ds(0, 1), :]
        place = position(code, routes.order(q, c))
        place = jnp.where((code >> routes.last(q, c)) & 1 == 1, place, wide)
        return jnp.broadcast_to(place, (n, width))

    def choose(ref, count, place):
        value = ref[0]
        for p in range(1, count):
            value = jnp.where(place == p, ref[p], value)
        return value

    def start_step(it, q, c, level):
        ref = gathered(it, q, c)
        count = 1 << level
        send(
            ("gather", it, q, c, level), ref.at[pl.ds(0, count)], ref.at[pl.ds(count, count)],
            wide_peer(1 << routes.order(q, c)[level]),
        )

    def start_back(it, q, c, level):
        count = 1 << level
        send(
            ("back", it, q, c, level), put_ref(it, q, c).at[pl.ds(count, count)],
            back_ref(it, q, c).at[pl.ds(count, count)], wide_peer(1 << routes.order(q, c)[level]),
        )

    def do_load(chunk):
        fetch(chunk).wait()
        hi, lo = split(stage[chunk % stages])
        at = pl.ds(chunk * stage_rows, stage_rows)
        tile_hi[at, :] = hi
        tile_lo[at, :] = lo
        turn_hi[:, at] = hi.T
        turn_lo[:, at] = lo.T
        if chunk + stages < LOAD_CHUNKS:
            fetch(chunk + stages).start()

    def do_turn(it):
        if slots == ITERS:
            return
        all_gone()
        for peer in peers:
            pl.semaphore_signal(fence_sem, inc=1, device_id=peer, device_id_type=MESH)
        pl.semaphore_wait(fence_sem, len(peers))
        for c in range(cuts):
            row_ref(it, 0, c)[...] = product[pl.ds(c * n, n), :]

    def do_have(it, q, c):
        ref = row_ref(it, q, c)
        if q > 0:
            received(("rows", it, q, c))
        elif it == 0:
            ref[...] = start[pl.ds(c * n, n), :]
        for child in routes.children(q):
            send(("rows", it, child, c), ref, row_ref(it, child, c), near_peer(child ^ q))
        if not (routes.paired(q, c) and q % 2 == 1):
            start_step(it, q, c, 0)
        keep_split(rows_right, piece_at(q, c), ref[...])

    def do_step(it, q, c, level):
        received(("gather", it, q, c, level - 1))
        start_step(it, q, c, level)

    def do_pick(it, q, c):
        levels = len(routes.order(q, c))
        received(("gather", it, q, c, levels - 1))
        if routes.paired(q, c):
            at = whole_at[q, c]
            picks[here(it), at] = choose(gathered(it, q, c), wide, position(mate_want, routes.order(q, c)))
            send(("pick", it, q, c), picks.at[here(it), at], picked.at[here(it), at], near_peer(1))
        else:
            at = half_at[q, c]
            choices[here(it), at] = choose(gathered(it, q, c), wide // 2, far_codes(q, c))
            send(
                ("pick", it, q, c), choices.at[here(it), at], chosen.at[here(it), at],
                wide_peer(1 << routes.last(q, c)),
            )

    def do_column(it, q, c):
        if routes.paired(q, c):
            if q % 2 == 0:
                value = choose(gathered(it, q, c), wide, position(own_want, routes.order(q, c)))
            else:
                received(("pick", it, q - 1, c))
                value = picked[here(it), whole_at[q - 1, c]]
        else:
            received(("pick", it, q, c))
            value = choose(gathered(it, q, c), wide // 2, position(own_want, routes.order(q, c)))
            value = jnp.where((own_want >> routes.last(q, c)) & 1 == 1, chosen[here(it), half_at[q, c]], value)
        keep_split(columns_right, piece_at(q, c), value)

    def product_of(hi, lo, right, at):
        both = jnp.dot(hi[at, :], right[...], preferred_element_type=f32)
        rest = jnp.dot(lo[at, :], right[:, pl.ds(0, width)], preferred_element_type=f32)
        return both[:, :width] + (both[:, width:] + rest)

    def do_trans(it, q):
        at = pl.ds(natural(q), rows)
        trans[here(it), at, :] = product_of(turn_hi, turn_lo, rows_right, at)

    def do_direct(it, q):
        at = pl.ds(natural(q), rows)
        direct[at, :] = product_of(tile_hi, tile_lo, columns_right, at)

    def do_pass(it, q, c):
        source = trans.at[here(it), piece_at(q, c)]
        if routes.paired(q, c):
            send(("pass", it, q, c), source, passed_mate.at[here(it), whole_at[q - 1, c]], near_peer(1))
        else:
            send(
                ("pass", it, q, c), source, passed.at[here(it), half_at[q, c]],
                wide_peer(1 << routes.last(q, c)),
            )

    def do_put(it, q, c):
        mine = trans[here(it), piece_at(q, c), :]
        ref = put_ref(it, q, c)
        places = routes.order(q, c)
        if routes.paired(q, c):
            received(("pass", it, q + 1, c))
            other = passed_mate[here(it), whole_at[q, c]]
            count, first, second = wide, position(own_want, places), position(mate_want, places)
        else:
            received(("pass", it, q, c))
            other = passed[here(it), half_at[q, c]]
            count, second = wide // 2, far_codes(q, c)
            first = position(own_want, places) + wide * ((own_want >> routes.last(q, c)) & 1)
        for p in range(count):
            ref[p] = jnp.where(first == p, mine, 0.0) + jnp.where(second == p, other, 0.0)
        start_back(it, q, c, len(places) - 1)

    def do_down(it, q, c, level):
        received(("back", it, q, c, level))
        count = 1 << level
        ref, came = put_ref(it, q, c), back_ref(it, q, c)
        for p in range(count):
            ref[p] = ref[p] + came[count + p]
        start_back(it, q, c, level - 1)

    def do_merge(it, q, c):
        value = direct[piece_at(q, c), :]
        if not (routes.paired(q, c) and q % 2 == 1):
            received(("back", it, q, c, 0))
            value = value + (put_ref(it, q, c)[0] + back_ref(it, q, c)[1])
        for child in routes.children(q):
            received(("part", it, child, c))
            value = value + part_in[here(it), child - 1, c]
        if q > 0:
            bit = 1 << lowest(q, routes.nbits)
            part[here(it), q - 1, c] = value
            send(("part", it, q, c), part.at[here(it), q - 1, c], part_in.at[here(it), q - 1, c], near_peer(bit))
        elif it < ITERS - 1:
            product[pl.ds(c * n, n), :] = value
            if slots == ITERS:
                row_ref(it + 1, 0, c)[...] = value
        else:
            product[pl.ds(c * n, n), :] = jnp.dot(value, roots[it - 1], precision=HIGHEST)

    grams_begun = set()

    def do_gram(it, c):
        value = product[pl.ds(c * n, n), :]
        square = lax.dot_general(value, value, (((0,), (0,)), ((), ())), precision=HIGHEST, preferred_element_type=f32)
        if it in grams_begun:
            grams[it] = grams[it] + square
        else:
            grams[it] = square
        grams_begun.add(it)

    def slice_of(mask):
        return pl.ds(pl.multiple_of(flip(me_w, mask) * slice_rows, slice_rows), slice_rows)

    def do_spread(it):
        for mask in range(1, wide):
            send(("spread", it, mask), grams.at[it, slice_of(mask)], gram_in.at[it, mask], wide_peer(mask))

    def do_sum(it):
        values = [grams[it, slice_of(0), :]]
        for mask in range(1, wide):
            received(("spread", it, mask))
            values.append(gram_in[it, mask])
        gram_sum[it] = tree_sum(values)
        for mask in range(1, narrow):
            send(("near", it, mask), gram_sum.at[it], gram_near.at[it, mask], near_peer(mask))

    def do_all(it):
        values = [gram_sum[it]]
        for mask in range(1, narrow):
            received(("near", it, mask))
            values.append(gram_near[it, mask])
        gram_part[it] = tree_sum(values)
        for mask in range(1, wide):
            send(("all", it, mask), gram_part.at[it], gram_all.at[it, slice_of(0)], wide_peer(mask))
        gram_all[it, slice_of(0), :] = gram_part[it]

    def identity():
        row = lax.broadcasted_iota(jnp.int32, (width, width), 0)
        column = lax.broadcasted_iota(jnp.int32, (width, width), 1)
        return jnp.where(row == column, 1.0, 0.0).astype(f32)

    def do_root(it, repeat):
        if repeat == 0:
            for mask in range(1, wide):
                received(("all", it, mask))
            gram = gram_all[it]
            square = jnp.sum(gram * gram, axis=1, keepdims=True)
            scale = jnp.sqrt(jnp.sum(square, axis=0, keepdims=True) + 1e-06)
            current = gram / scale
            middle = 1.5 * identity() - 0.5 * current
            inverse = middle
            ns[2] = jnp.broadcast_to(jnp.sqrt(total_rows / scale), (width, width))
        else:
            current, inverse = ns[0], ns[1]
            middle = 1.5 * identity() - 0.5 * jnp.dot(inverse, current, precision=HIGHEST)
            inverse = jnp.dot(middle, inverse, precision=HIGHEST)
        if repeat < NS_STEPS - 1:
            ns[0] = jnp.dot(current, middle, precision=HIGHEST)
            ns[1] = inverse
        else:
            roots[it] = inverse * ns[2]

    actions = dict(
        load=do_load, turn=do_turn, have=do_have, step=do_step, pick=do_pick, column=do_column, trans=do_trans,
        direct=do_direct, put=do_put, down=do_down, merge=do_merge, gram=do_gram, spread=do_spread, sum=do_sum,
        all=do_all, root=do_root,
    )
    actions["pass"] = do_pass
    for name in sequence:
        actions[name[0]](*name[1:])
    out[...] = jnp.dot(product[...], roots[ITERS - 1], precision=HIGHEST)
    all_gone()


def on_device(hamiltonian_tiles, row_columns, start_vectors):
    wide, narrow = lax.axis_size("wide"), lax.axis_size("narrow")
    order = hamiltonian_tiles.shape[0]
    rows, width = start_vectors.shape
    assert rows * narrow == order
    routes = Routes(wide, narrow)
    cuts = routes.cuts
    n = rows // cuts
    slots = ITERS if narrow <= 4 else 1
    sequence = steps_of(routes)
    if len(ORDER) == len(sequence):
        sequence = [sequence[place] for place in ORDER]
    copies = sends_of(routes)
    wholes, halves = max(1, len(routes.whole)), max(1, len(routes.half))
    f32, bf16 = jnp.float32, jnp.bfloat16
    stage_rows = order // LOAD_CHUNKS
    slice_rows = width // wide

    def vmem(*shape, dtype=f32):
        return pltpu.VMEM(shape, dtype)

    return pl.pallas_call(
        functools.partial(kernel, routes, sequence, slots),
        out_shape=jax.ShapeDtypeStruct((rows, width), f32),
        in_specs=[
            pl.BlockSpec(memory_space=pltpu.SMEM),
            pl.BlockSpec(memory_space=pl.ANY),
            pl.BlockSpec(memory_space=pltpu.VMEM),
        ],
        out_specs=pl.BlockSpec(memory_space=pltpu.VMEM),
        scratch_shapes=[
            vmem(2, stage_rows, order),
            vmem(order, order, dtype=bf16),
            vmem(order, order, dtype=bf16),
            vmem(order, order, dtype=bf16),
            vmem(order, order, dtype=bf16),
            vmem(order, 2 * width, dtype=bf16),
            vmem(order, 2 * width, dtype=bf16),
            vmem(slots, order, width),
            vmem(order, width),
            vmem(slots, wholes, wide, n, width),
            vmem(slots, halves, wide // 2, n, width),
            vmem(slots, wholes, n, width),
            vmem(slots, wholes, n, width),
            vmem(slots, wholes, n, width),
            vmem(slots, halves, n, width),
            vmem(slots, halves, n, width),
            vmem(slots, wholes, wide, n, width),
            vmem(slots, halves, wide // 2, n, width),
            vmem(slots, wholes, wide, n, width),
            vmem(slots, halves, wide // 2, n, width),
            vmem(slots, halves, n, width),
            vmem(slots, wholes, n, width),
            vmem(slots, narrow - 1, cuts, n, width),
            vmem(slots, narrow - 1, cuts, n, width),
            vmem(rows, width),
            vmem(8, 128, dtype=jnp.int32),
            vmem(2, 8, 128, dtype=jnp.int32),
            vmem(ITERS, width, width),
            vmem(ITERS, wide, slice_rows, width),
            vmem(ITERS, slice_rows, width),
            vmem(ITERS, narrow, slice_rows, width),
            vmem(ITERS, slice_rows, width),
            vmem(ITERS, width, width),
            vmem(3, width, width),
            vmem(ITERS, width, width),
            pltpu.SemaphoreType.DMA((2,)),
            pltpu.SemaphoreType.DMA((copies,)),
            pltpu.SemaphoreType.DMA((copies,)),
            pltpu.SemaphoreType.REGULAR,
        ],
        compiler_params=pltpu.CompilerParams(
            collective_id=0, has_side_effects=True, vmem_limit_bytes=67043328
        ),
    )(row_columns, hamiltonian_tiles, start_vectors)


def solution(mesh):
    return jax.shard_map(
        on_device,
        mesh=mesh,
        in_specs=(P("wide", "narrow"), P("wide", None), P(("wide", "narrow"), None)),
        out_specs=P(("wide", "narrow"), None),
        check_vma=False,
    )
```

time: 142 us -> 106 us (0.75)
  Pallas kernels: 138 us -> 105 us
    pallas_call x1, Pallas kernels: 138 us -> 105 us  [on_device(): pl.pallas_call(functools.partial(kernel, routes, sequence, slots), out_sh...]
where the time goes in v1:
time: 106 us
  Pallas kernels  105 us (99%)
  local copies, waits for them, and re-layouts  1.62 us (2%)
    pallas_call x1, Pallas kernels, on_device(): pl.pallas_call(functools.partial(kernel, routes, sequence, slots), out_sh...  105 us

profile of v1, /device:TPU:0, one launch (start us, length us, event | category | flops | bytes accessed | tf_op | source)
XLA Modules:
  0.0 106.3 jit_solution(473199380770868926)
XLA Ops:
  0.0 104.6 %shard_map.37 = f32[384,128]{1,0:T(8,128)} custom-call(s32[1,4]{1,0:T(1,128)} %row_columns.1, f32[1536,1536]{1,0:T(8,128)} %tile_hbm.1, f32[384,128]{1,0:T(8,128)} %start.1), custom_call_target="tpu_custom_call" | custom-call | tf_op jit(solution)/shard_map/pallas_call | solution.py:537
  104.6 1.6 %copy.5 = f32[384,128]{1,0:T(8,128)} copy(f32[384,128]{1,0:T(8,128)} %shard_map.37) | data formatting | bytes 393216

commit v2 on v1

--- a/solution.py
+++ b/solution.py
@@ -8,23 +8,25 @@
 from jax.sharding import PartitionSpec as P
 
 ITERS = 2
+SHARES = 2
 NS_STEPS = 5
 HIGHEST = lax.Precision.HIGHEST
 MESH = pl.DeviceIdType.MESH
 LOAD_CHUNKS = 6
 ORDER = (
-    7, 8, 9, 0, 6, 23, 15, 1, 134, 11, 24, 16, 25, 2, 17, 3, 35, 27, 28, 22, 14, 44, 43, 36,
-    19, 4, 12, 5, 39, 20, 26, 10, 13, 21, 18, 55, 57, 59, 29, 31, 56, 50, 51, 52, 67, 54, 53, 40,
-    32, 60, 62, 61, 45, 30, 34, 37, 65, 42, 48, 46, 38, 66, 33, 68, 47, 87, 41, 69, 75, 86, 63, 49,
-    89, 95, 90, 103, 91, 94, 105, 77, 102, 70, 76, 74, 88, 107, 58, 99, 71, 80, 64, 72, 73, 81, 78, 79,
-    82, 115, 93, 106, 117, 104, 114, 84, 122, 83, 97, 109, 98, 119, 116, 111, 92, 118, 96, 108, 123, 101, 100, 121,
-    124, 120, 110, 125, 85, 127, 113, 112, 136, 126, 135, 129, 138, 128, 137, 130, 152, 144, 132, 151, 143, 131, 154, 153,
-    133, 156, 172, 146, 163, 164, 243, 145, 155, 167, 148, 141, 168, 166, 165, 147, 196, 171, 170, 139, 140, 158, 198, 150,
-    244, 149, 142, 179, 183, 180, 169, 157, 181, 182, 159, 160, 189, 191, 184, 185, 174, 162, 161, 190, 175, 176, 194, 218,
-    215, 178, 177, 195, 173, 188, 217, 200, 234, 216, 193, 231, 192, 219, 199, 201, 223, 187, 203, 208, 233, 197, 186, 202,
-    245, 209, 210, 227, 207, 204, 235, 205, 206, 211, 251, 226, 224, 254, 222, 232, 220, 213, 259, 238, 228, 221, 225, 253,
-    212, 255, 236, 237, 239, 252, 229, 258, 230, 261, 240, 246, 247, 257, 260, 248, 249, 250, 256, 241, 262, 214, 263, 267,
-    242, 265, 269, 264, 268, 266, 270, 271, 272, 273, 274, 275, 276, 277, 278,
+    9, 8, 7, 0, 1, 25, 2, 17, 23, 24, 3, 4, 13, 16, 5, 6, 37, 11, 12, 29, 15, 41, 73, 21,
+    45, 35, 36, 20, 51, 54, 55, 63, 67, 22, 57, 60, 14, 61, 10, 28, 66, 19, 40, 33, 39, 32, 69, 44,
+    72, 97, 140, 96, 49, 77, 105, 48, 113, 18, 62, 68, 50, 64, 76, 65, 112, 53, 81, 101, 80, 109, 84, 85,
+    87, 125, 117, 104, 100, 52, 56, 31, 124, 108, 116, 91, 133, 30, 89, 129, 121, 59, 27, 47, 34, 46, 132, 95,
+    93, 58, 128, 71, 94, 26, 120, 43, 38, 70, 103, 111, 42, 137, 144, 110, 99, 102, 107, 75, 83, 98, 115, 136,
+    143, 82, 79, 74, 78, 86, 123, 114, 106, 160, 122, 152, 92, 151, 88, 127, 119, 90, 131, 148, 147, 159, 126, 118,
+    156, 130, 164, 155, 186, 190, 189, 192, 196, 163, 135, 142, 180, 139, 204, 179, 171, 168, 195, 134, 141, 231, 198, 167,
+    236, 172, 158, 184, 201, 138, 232, 150, 257, 215, 216, 157, 183, 235, 146, 252, 149, 175, 176, 251, 202, 220, 239, 170,
+    247, 207, 248, 145, 208, 162, 154, 258, 174, 206, 219, 153, 203, 185, 161, 211, 188, 187, 197, 199, 191, 200, 212, 169,
+    177, 178, 222, 268, 165, 173, 267, 166, 193, 205, 230, 229, 194, 226, 275, 182, 181, 240, 238, 246, 245, 224, 237, 243,
+    244, 272, 214, 210, 233, 276, 209, 213, 218, 217, 221, 265, 241, 249, 266, 271, 234, 242, 225, 250, 273, 223, 259, 269,
+    255, 256, 274, 228, 227, 253, 270, 254, 260, 261, 280, 262, 263, 264, 277, 279, 281, 278, 282, 283, 284, 285, 286, 287,
+    288, 289, 290,
 )
 
 
@@ -43,10 +45,6 @@
     return bits
 
 
-def lowest(q, bits):
-    return bits if q == 0 else (q & -q).bit_length() - 1
-
-
 def position(relative, order):
     return sum(((relative >> bit) & 1) << place for place, bit in enumerate(order))
 
@@ -55,7 +53,8 @@
     def __init__(self, wide, narrow):
         self.wide, self.narrow = wide, narrow
         self.wbits, self.nbits = bits_of(wide), bits_of(narrow)
-        self.cuts = max(1, 4 * 4 // narrow)
+        self.cuts = max(SHARES, 4 * 4 // narrow)
+        self.run = self.cuts // SHARES
         upper = list(range(1, self.wbits))
         self.lines = [upper, upper[::-1]]
         self.whole = []
@@ -71,6 +70,9 @@
     def side(self, q, c):
         return (q + c) % 2
 
+    def share(self, c):
+        return c // self.run
+
     def paired(self, q, c):
         return q < 2
 
@@ -81,8 +83,14 @@
     def last(self, q, c):
         return self.lines[self.side(q, c)][-1]
 
-    def children(self, q):
-        return [q | (1 << b) for b in range(lowest(q, self.nbits) - 1, -1, -1)]
+    def straight(self, c):
+        return False
+
+    def parent(self, q, c):
+        return 0 if self.straight(c) else q & (q - 1)
+
+    def children(self, q, c):
+        return [other for other in range(self.narrow - 1, 0, -1) if self.parent(other, c) == q]
 
 
 def steps_of(routes):
@@ -107,7 +115,8 @@
                 if not (routes.paired(q, c) and q % 2 == 1):
                     steps.append(("pick", it, q, c))
         for q in quarters[::-1]:
-            steps.append(("trans", it, q))
+            for share in range(SHARES):
+                steps.append(("trans", it, q, share))
             for c in cuts:
                 if not (routes.paired(q, c) and q % 2 == 0):
                     steps.append(("pass", it, q, c))
@@ -115,7 +124,8 @@
             for c in cuts:
                 steps.append(("column", it, q, c))
         for q in quarters[::-1]:
-            steps.append(("direct", it, q))
+            for share in range(SHARES):
+                steps.append(("direct", it, q, share))
         for q in quarters[::-1]:
             for c in cuts:
                 if not (routes.paired(q, c) and q % 2 == 1):
@@ -135,7 +145,7 @@
         for q in quarters[::-1]:
             for c in cuts:
                 steps.append(("merge", it, q, c))
-        for c in cuts:
+        for c in range(routes.run):
             steps.append(("gram", it, c))
     steps.append(("spread", ITERS - 1))
     steps.append(("sum", ITERS - 1))
@@ -169,7 +179,7 @@
 
 def kernel(routes, sequence, slots, row_columns, tile_hbm, start, out, stage, tile_hi, tile_lo, turn_hi, turn_lo,
            rows_right, columns_right, trans, direct, whole_in, half_in, mate_rows, picks, picked, choices, chosen,
-           whole_put, half_put, whole_back, half_back, passed, passed_mate, part, part_in, product, want, wants,
+           whole_put, half_put, whole_back, half_back, passed, passed_mate, part, part_in, product, turned, want, wants,
            grams, gram_in, gram_sum, gram_near, gram_part, gram_all, ns, roots,
            stage_sem, send_sem, recv_sem, fence_sem):
     wide, narrow, cuts = routes.wide, routes.narrow, routes.cuts
@@ -182,6 +192,9 @@
     f32 = jnp.float32
     slice_rows = width // wide
     total_rows = float(wide * order)
+    run = routes.run
+    half_width = width // SHARES
+    first_lanes = lax.broadcasted_iota(jnp.int32, (n, width), 1) < half_width
     whole_at = {unit: place for place, unit in enumerate(routes.whole)}
     half_at = {unit: place for place, unit in enumerate(routes.half)}
 
@@ -244,8 +257,12 @@
     def natural(q):
         return pl.multiple_of(flip(me_z, q) * rows, rows)
 
-    def piece_at(q, c):
-        return pl.ds(pl.multiple_of(natural(q) + c * n, n), n)
+    def swap(x):
+        return pltpu.roll(x, half_width, 1)
+
+    def rows_of(c):
+        at = (c % run) * 2 * n
+        return at, at + n
 
     def here(it):
         return it % slots
@@ -270,10 +287,14 @@
             return whole_back.at[here(it), whole_at[q, c]]
         return half_back.at[here(it), half_at[q, c]]
 
-    def keep_split(target, at, value):
-        hi, lo = split(value)
-        target[at, pl.ds(0, width)] = hi
-        target[at, pl.ds(width, width)] = lo
+    def keep_split(target, q, c, value):
+        hi = value.astype(jnp.bfloat16).astype(f32)
+        lo = value - hi
+        first, second = rows_of(c)
+        at = pl.ds(pl.multiple_of(natural(q) + first, n), n)
+        target[routes.share(c), at, :] = jnp.where(first_lanes, hi, swap(lo)).astype(jnp.bfloat16)
+        at = pl.ds(pl.multiple_of(natural(q) + second, n), n)
+        target[routes.share(c), at, :] = jnp.where(first_lanes, swap(hi), lo).astype(jnp.bfloat16)
 
     def far_codes(q, c):
         side = routes.side(q, c)
@@ -325,19 +346,23 @@
             pl.semaphore_signal(fence_sem, inc=1, device_id=peer, device_id_type=MESH)
         pl.semaphore_wait(fence_sem, len(peers))
         for c in range(cuts):
-            row_ref(it, 0, c)[...] = product[pl.ds(c * n, n), :]
+            row_ref(it, 0, c)[...] = product[c]
 
     def do_have(it, q, c):
         ref = row_ref(it, q, c)
         if q > 0:
             received(("rows", it, q, c))
         elif it == 0:
-            ref[...] = start[pl.ds(c * n, n), :]
-        for child in routes.children(q):
+            first, second = (start[pl.ds(at, n), :] for at in rows_of(c))
+            if routes.share(c) == 0:
+                ref[...] = jnp.where(first_lanes, first, swap(second))
+            else:
+                ref[...] = jnp.where(first_lanes, swap(first), second)
+        for child in routes.children(q, c):
             send(("rows", it, child, c), ref, row_ref(it, child, c), near_peer(child ^ q))
         if not (routes.paired(q, c) and q % 2 == 1):
             start_step(it, q, c, 0)
-        keep_split(rows_right, piece_at(q, c), ref[...])
+        keep_split(rows_right, q, c, ref[...])
 
     def do_step(it, q, c, level):
         received(("gather", it, q, c, level - 1))
@@ -369,23 +394,25 @@
             received(("pick", it, q, c))
             value = choose(gathered(it, q, c), wide // 2, position(own_want, routes.order(q, c)))
             value = jnp.where((own_want >> routes.last(q, c)) & 1 == 1, chosen[here(it), half_at[q, c]], value)
-        keep_split(columns_right, piece_at(q, c), value)
-
-    def product_of(hi, lo, right, at):
-        both = jnp.dot(hi[at, :], right[...], preferred_element_type=f32)
-        rest = jnp.dot(lo[at, :], right[:, pl.ds(0, width)], preferred_element_type=f32)
-        return both[:, :width] + (both[:, width:] + rest)
-
-    def do_trans(it, q):
+        keep_split(columns_right, q, c, value)
+
+    def product_of(target, q, share, hi, lo, right):
         at = pl.ds(natural(q), rows)
-        trans[here(it), at, :] = product_of(turn_hi, turn_lo, rows_right, at)
-
-    def do_direct(it, q):
-        at = pl.ds(natural(q), rows)
-        direct[at, :] = product_of(tile_hi, tile_lo, columns_right, at)
+        value = jnp.dot(hi[at, :], right[share], preferred_element_type=f32)
+        value = value + jnp.dot(lo[at, :], right[share], preferred_element_type=f32)
+        value = value + swap(value)
+        for c in range(share * run, (share + 1) * run):
+            first, second = rows_of(c)
+            target[q, c] = jnp.where(first_lanes, value[first:first + n], value[second:second + n])
+
+    def do_trans(it, q, share):
+        product_of(trans.at[here(it)], q, share, turn_hi, turn_lo, rows_right)
+
+    def do_direct(it, q, share):
+        product_of(direct, q, share, tile_hi, tile_lo, columns_right)
 
     def do_pass(it, q, c):
-        source = trans.at[here(it), piece_at(q, c)]
+        source = trans.at[here(it), q, c]
         if routes.paired(q, c):
             send(("pass", it, q, c), source, passed_mate.at[here(it), whole_at[q - 1, c]], near_peer(1))
         else:
@@ -395,7 +422,7 @@
             )
 
     def do_put(it, q, c):
-        mine = trans[here(it), piece_at(q, c), :]
+        mine = trans[here(it), q, c]
         ref = put_ref(it, q, c)
         places = routes.order(q, c)
         if routes.paired(q, c):
@@ -420,28 +447,32 @@
         start_back(it, q, c, level - 1)
 
     def do_merge(it, q, c):
-        value = direct[piece_at(q, c), :]
+        value = direct[q, c]
         if not (routes.paired(q, c) and q % 2 == 1):
             received(("back", it, q, c, 0))
             value = value + (put_ref(it, q, c)[0] + back_ref(it, q, c)[1])
-        for child in routes.children(q):
+        for child in routes.children(q, c):
             received(("part", it, child, c))
             value = value + part_in[here(it), child - 1, c]
         if q > 0:
-            bit = 1 << lowest(q, routes.nbits)
             part[here(it), q - 1, c] = value
-            send(("part", it, q, c), part.at[here(it), q - 1, c], part_in.at[here(it), q - 1, c], near_peer(bit))
-        elif it < ITERS - 1:
-            product[pl.ds(c * n, n), :] = value
-            if slots == ITERS:
+            send(("part", it, q, c), part.at[here(it), q - 1, c], part_in.at[here(it), q - 1, c],
+                 near_peer(q ^ routes.parent(q, c)))
+        else:
+            product[c] = value
+            if it < ITERS - 1 and slots == ITERS:
                 row_ref(it + 1, 0, c)[...] = value
-        else:
-            product[pl.ds(c * n, n), :] = jnp.dot(value, roots[it - 1], precision=HIGHEST)
 
     grams_begun = set()
 
     def do_gram(it, c):
-        value = product[pl.ds(c * n, n), :]
+        left, right = product[c], product[run + c]
+        value = jnp.concatenate(
+            [jnp.where(first_lanes, left, swap(right)), jnp.where(first_lanes, swap(left), right)], axis=0
+        )
+        if it > 0:
+            value = jnp.dot(value, roots[it - 1], precision=HIGHEST)
+            turned[pl.ds(c * 2 * n, 2 * n), :] = value
         square = lax.dot_general(value, value, (((0,), (0,)), ((), ())), precision=HIGHEST, preferred_element_type=f32)
         if it in grams_begun:
             grams[it] = grams[it] + square
@@ -509,7 +540,7 @@
     actions["pass"] = do_pass
     for name in sequence:
         actions[name[0]](*name[1:])
-    out[...] = jnp.dot(product[...], roots[ITERS - 1], precision=HIGHEST)
+    out[...] = jnp.dot(turned[...], roots[ITERS - 1], precision=HIGHEST)
     all_gone()
 
 
@@ -549,10 +580,10 @@
             vmem(order, order, dtype=bf16),
             vmem(order, order, dtype=bf16),
             vmem(order, order, dtype=bf16),
-            vmem(order, 2 * width, dtype=bf16),
-            vmem(order, 2 * width, dtype=bf16),
-            vmem(slots, order, width),
-            vmem(order, width),
+            vmem(SHARES, order, width, dtype=bf16),
+            vmem(SHARES, order, width, dtype=bf16),
+            vmem(slots, narrow, cuts, n, width),
+            vmem(narrow, cuts, n, width),
             vmem(slots, wholes, wide, n, width),
             vmem(slots, halves, wide // 2, n, width),
             vmem(slots, wholes, n, width),
@@ -568,6 +599,7 @@
             vmem(slots, wholes, n, width),
             vmem(slots, narrow - 1, cuts, n, width),
             vmem(slots, narrow - 1, cuts, n, width),
+            vmem(cuts, n, width),
             vmem(rows, width),
             vmem(8, 128, dtype=jnp.int32),
             vmem(2, 8, 128, dtype=jnp.int32),

time: 106 us -> 107 us (level)
  no operation moved by 1% of the time
where the time goes in v2:
time: 107 us
  Pallas kernels  105 us (98%)
  local copies, waits for them, and re-layouts  1.62 us (2%)
    pallas_call x1, Pallas kernels, on_device(): pl.pallas_call(functools.partial(kernel, routes, sequence, slots), out_sh...  105 us

profile of v2, /device:TPU:0, one launch (start us, length us, event | category | flops | bytes accessed | tf_op | source)
XLA Modules:
  0.0 107.1 jit_solution(2131933580286969124)
XLA Ops:
  0.0 105.5 %shard_map.37 = f32[384,128]{1,0:T(8,128)} custom-call(s32[1,4]{1,0:T(1,128)} %row_columns.1, f32[1536,1536]{1,0:T(8,128)} %tile_hbm.1, f32[384,128]{1,0:T(8,128)} %start.1), custom_call_target="tpu_custom_call" | custom-call | tf_op jit(solution)/shard_map/pallas_call | solution.py:568
  105.5 1.6 %copy.5 = f32[384,128]{1,0:T(8,128)} copy(f32[384,128]{1,0:T(8,128)} %shard_map.37) | data formatting | bytes 393216

commit v3 on v2

--- a/solution.py
+++ b/solution.py
@@ -12,21 +12,21 @@
 NS_STEPS = 5
 HIGHEST = lax.Precision.HIGHEST
 MESH = pl.DeviceIdType.MESH
-LOAD_CHUNKS = 6
+LOAD_CHUNKS = 12
 ORDER = (
-    9, 8, 7, 0, 1, 25, 2, 17, 23, 24, 3, 4, 13, 16, 5, 6, 37, 11, 12, 29, 15, 41, 73, 21,
-    45, 35, 36, 20, 51, 54, 55, 63, 67, 22, 57, 60, 14, 61, 10, 28, 66, 19, 40, 33, 39, 32, 69, 44,
-    72, 97, 140, 96, 49, 77, 105, 48, 113, 18, 62, 68, 50, 64, 76, 65, 112, 53, 81, 101, 80, 109, 84, 85,
-    87, 125, 117, 104, 100, 52, 56, 31, 124, 108, 116, 91, 133, 30, 89, 129, 121, 59, 27, 47, 34, 46, 132, 95,
-    93, 58, 128, 71, 94, 26, 120, 43, 38, 70, 103, 111, 42, 137, 144, 110, 99, 102, 107, 75, 83, 98, 115, 136,
-    143, 82, 79, 74, 78, 86, 123, 114, 106, 160, 122, 152, 92, 151, 88, 127, 119, 90, 131, 148, 147, 159, 126, 118,
-    156, 130, 164, 155, 186, 190, 189, 192, 196, 163, 135, 142, 180, 139, 204, 179, 171, 168, 195, 134, 141, 231, 198, 167,
-    236, 172, 158, 184, 201, 138, 232, 150, 257, 215, 216, 157, 183, 235, 146, 252, 149, 175, 176, 251, 202, 220, 239, 170,
-    247, 207, 248, 145, 208, 162, 154, 258, 174, 206, 219, 153, 203, 185, 161, 211, 188, 187, 197, 199, 191, 200, 212, 169,
-    177, 178, 222, 268, 165, 173, 267, 166, 193, 205, 230, 229, 194, 226, 275, 182, 181, 240, 238, 246, 245, 224, 237, 243,
-    244, 272, 214, 210, 233, 276, 209, 213, 218, 217, 221, 265, 241, 249, 266, 271, 234, 242, 225, 250, 273, 223, 259, 269,
-    255, 256, 274, 228, 227, 253, 270, 254, 260, 261, 280, 262, 263, 264, 277, 279, 281, 278, 282, 283, 284, 285, 286, 287,
-    288, 289, 290,
+    146, 15, 0, 1, 12, 2, 14, 3, 4, 5, 6, 23, 31, 13, 7, 8, 30, 22, 20, 9, 35, 28, 27, 29,
+    16, 43, 18, 10, 11, 21, 42, 19, 26, 57, 61, 60, 69, 72, 63, 66, 46, 39, 24, 34, 25, 17, 62, 47,
+    73, 38, 67, 50, 51, 41, 55, 75, 102, 110, 68, 70, 54, 56, 118, 103, 58, 36, 32, 40, 114, 33, 71, 78,
+    106, 37, 119, 45, 74, 52, 107, 44, 76, 53, 122, 86, 83, 82, 59, 91, 65, 79, 87, 90, 93, 130, 111, 131,
+    49, 123, 97, 139, 109, 48, 126, 115, 100, 138, 108, 89, 95, 77, 116, 134, 80, 64, 112, 135, 88, 85, 81, 101,
+    84, 96, 136, 105, 137, 92, 117, 128, 127, 104, 99, 142, 149, 120, 94, 98, 121, 113, 129, 143, 150, 132, 124, 165,
+    157, 166, 125, 133, 158, 169, 140, 147, 144, 185, 177, 161, 153, 141, 148, 154, 162, 192, 196, 195, 198, 170, 202, 201,
+    163, 155, 178, 204, 207, 173, 186, 156, 152, 189, 145, 182, 174, 263, 181, 213, 159, 242, 238, 190, 164, 167, 210, 151,
+    245, 214, 241, 208, 237, 175, 160, 203, 205, 183, 191, 194, 193, 179, 221, 254, 264, 253, 168, 171, 197, 199, 176, 258,
+    184, 187, 200, 225, 257, 206, 172, 209, 243, 218, 180, 226, 235, 217, 188, 219, 222, 228, 273, 274, 251, 236, 215, 232,
+    239, 265, 249, 244, 252, 220, 282, 230, 281, 223, 255, 216, 212, 224, 211, 227, 271, 277, 246, 248, 247, 240, 229, 256,
+    272, 278, 250, 261, 266, 267, 268, 275, 231, 260, 279, 276, 259, 262, 280, 269, 270, 234, 285, 233, 283, 287, 286, 284,
+    288, 289, 290, 291, 292, 293, 294, 295, 296,
 )
 
 
@@ -171,17 +171,28 @@
     return high, low
 
 
+def split_dot(a, b):
+    a_high, a_low = split(a)
+    b_high, b_low = split(b)
+    left = jnp.concatenate([a_high, a_low], axis=1)
+    right = jnp.concatenate(
+        [jnp.concatenate([b_high, b_low], axis=1), jnp.concatenate([b_high, jnp.zeros_like(b_low)], axis=1)], axis=0
+    )
+    both = jnp.dot(left, right, preferred_element_type=jnp.float32)
+    return both[:, : b.shape[1]] + both[:, b.shape[1]:]
+
+
 def tree_sum(values):
     while len(values) > 1:
         values = [a + b for a, b in zip(values[::2], values[1::2])]
     return values[0]
 
 
-def kernel(routes, sequence, slots, row_columns, tile_hbm, start, out, stage, tile_hi, tile_lo, turn_hi, turn_lo,
+def kernel(routes, sequence, slots, row_columns, tile_hbm, start_hbm, out, start, stage, tile_hi, tile_lo, turn_hi, turn_lo,
            rows_right, columns_right, trans, direct, whole_in, half_in, mate_rows, picks, picked, choices, chosen,
            whole_put, half_put, whole_back, half_back, passed, passed_mate, part, part_in, product, turned, want, wants,
            grams, gram_in, gram_sum, gram_near, gram_part, gram_all, ns, roots,
-           stage_sem, send_sem, recv_sem, fence_sem):
+           stage_sem, start_sem, send_sem, recv_sem, fence_sem):
     wide, narrow, cuts = routes.wide, routes.narrow, routes.cuts
     me_w = lax.axis_index("wide")
     me_z = lax.axis_index("narrow")
@@ -219,6 +230,8 @@
             stage_sem.at[chunk % stages],
         )
 
+    begin = pltpu.make_async_copy(start_hbm, start, start_sem)
+    begin.start()
     for chunk in range(stages):
         fetch(chunk).start()
 
@@ -244,12 +257,13 @@
     def received(name):
         sent[name].wait_recv()
 
-    def all_gone():
+    def all_gone(*spared):
         for name, copy in sent.items():
-            if name not in waited:
+            if name not in waited and name[0] not in spared:
                 copy.wait_send()
                 waited.add(name)
 
+    begin.wait()
     for side in range(2):
         send(("want", side), want, wants.at[side], wide_peer(1 << routes.lines[side][-1]))
     wants_here = set()
@@ -471,7 +485,7 @@
             [jnp.where(first_lanes, left, swap(right)), jnp.where(first_lanes, swap(left), right)], axis=0
         )
         if it > 0:
-            value = jnp.dot(value, roots[it - 1], precision=HIGHEST)
+            value = split_dot(value, roots[it - 1])
             turned[pl.ds(c * 2 * n, 2 * n), :] = value
         square = lax.dot_general(value, value, (((0,), (0,)), ((), ())), precision=HIGHEST, preferred_element_type=f32)
         if it in grams_begun:
@@ -488,6 +502,8 @@
             send(("spread", it, mask), grams.at[it, slice_of(mask)], gram_in.at[it, mask], wide_peer(mask))
 
     def do_sum(it):
+        if it == ITERS - 1:
+            all_gone("spread")
         values = [grams[it, slice_of(0), :]]
         for mask in range(1, wide):
             received(("spread", it, mask))
@@ -497,6 +513,8 @@
             send(("near", it, mask), gram_sum.at[it], gram_near.at[it, mask], near_peer(mask))
 
     def do_all(it):
+        if it == ITERS - 1:
+            all_gone("near")
         values = [gram_sum[it]]
         for mask in range(1, narrow):
             received(("near", it, mask))
@@ -513,6 +531,8 @@
 
     def do_root(it, repeat):
         if repeat == 0:
+            if it == ITERS - 1:
+                all_gone("all")
             for mask in range(1, wide):
                 received(("all", it, mask))
             gram = gram_all[it]
@@ -524,10 +544,10 @@
             ns[2] = jnp.broadcast_to(jnp.sqrt(total_rows / scale), (width, width))
         else:
             current, inverse = ns[0], ns[1]
-            middle = 1.5 * identity() - 0.5 * jnp.dot(inverse, current, precision=HIGHEST)
-            inverse = jnp.dot(middle, inverse, precision=HIGHEST)
+            middle = 1.5 * identity() - 0.5 * split_dot(inverse, current)
+            inverse = split_dot(middle, inverse)
         if repeat < NS_STEPS - 1:
-            ns[0] = jnp.dot(current, middle, precision=HIGHEST)
+            ns[0] = split_dot(current, middle)
             ns[1] = inverse
         else:
             roots[it] = inverse * ns[2]
@@ -540,8 +560,8 @@
     actions["pass"] = do_pass
     for name in sequence:
         actions[name[0]](*name[1:])
-    out[...] = jnp.dot(turned[...], roots[ITERS - 1], precision=HIGHEST)
     all_gone()
+    out[...] = split_dot(turned[...], roots[ITERS - 1])
 
 
 def on_device(hamiltonian_tiles, row_columns, start_vectors):
@@ -571,10 +591,11 @@
         in_specs=[
             pl.BlockSpec(memory_space=pltpu.SMEM),
             pl.BlockSpec(memory_space=pl.ANY),
-            pl.BlockSpec(memory_space=pltpu.VMEM),
+            pl.BlockSpec(memory_space=pl.ANY),
         ],
         out_specs=pl.BlockSpec(memory_space=pltpu.VMEM),
         scratch_shapes=[
+            vmem(rows, width),
             vmem(2, stage_rows, order),
             vmem(order, order, dtype=bf16),
             vmem(order, order, dtype=bf16),
@@ -612,6 +633,7 @@
             vmem(3, width, width),
             vmem(ITERS, width, width),
             pltpu.SemaphoreType.DMA((2,)),
+            pltpu.SemaphoreType.DMA,
             pltpu.SemaphoreType.DMA((copies,)),
             pltpu.SemaphoreType.DMA((copies,)),
             pltpu.SemaphoreType.REGULAR,

time: 107 us -> 111 us (1.037)
  Pallas kernels: 105 us -> 109 us
    pallas_call x1, Pallas kernels: 105 us -> 109 us  [on_device(): pl.pallas_call(functools.partial(kernel, routes, sequence, slots), out_sh...]
where the time goes in v3:
time: 111 us
  Pallas kernels  109 us (98%)
  local copies, waits for them, and re-layouts  1.62 us (1%)
    pallas_call x1, Pallas kernels, on_device(): pl.pallas_call(functools.partial(kernel, routes, sequence, slots), out_sh...  109 us

profile of v3, /device:TPU:0, one launch (start us, length us, event | category | flops | bytes accessed | tf_op | source)
XLA Modules:
  0.0 111.1 jit_solution(11492433184128413240)
XLA Ops:
  0.0 109.5 %shard_map.37 = f32[384,128]{1,0:T(8,128)} custom-call(s32[1,4]{1,0:T(1,128)} %row_columns.1, f32[1536,1536]{1,0:T(8,128)} %tile_hbm.1, f32[384,128]{1,0:T(8,128)} %start_hbm.1), custom_call_target="tpu_custom_call" | custom-call | tf_op jit(solution)/shard_map/pallas_call | solution.py:588
  109.5 1.6 %copy.5 = f32[384,128]{1,0:T(8,128)} copy(f32[384,128]{1,0:T(8,128)} %shard_map.37) | data formatting | bytes 393216

commit v4 on v1

--- a/solution.py
+++ b/solution.py
@@ -11,20 +11,20 @@
 NS_STEPS = 5
 HIGHEST = lax.Precision.HIGHEST
 MESH = pl.DeviceIdType.MESH
-LOAD_CHUNKS = 6
+LOAD_CHUNKS = 12
 ORDER = (
-    7, 8, 9, 0, 6, 23, 15, 1, 134, 11, 24, 16, 25, 2, 17, 3, 35, 27, 28, 22, 14, 44, 43, 36,
-    19, 4, 12, 5, 39, 20, 26, 10, 13, 21, 18, 55, 57, 59, 29, 31, 56, 50, 51, 52, 67, 54, 53, 40,
-    32, 60, 62, 61, 45, 30, 34, 37, 65, 42, 48, 46, 38, 66, 33, 68, 47, 87, 41, 69, 75, 86, 63, 49,
-    89, 95, 90, 103, 91, 94, 105, 77, 102, 70, 76, 74, 88, 107, 58, 99, 71, 80, 64, 72, 73, 81, 78, 79,
-    82, 115, 93, 106, 117, 104, 114, 84, 122, 83, 97, 109, 98, 119, 116, 111, 92, 118, 96, 108, 123, 101, 100, 121,
-    124, 120, 110, 125, 85, 127, 113, 112, 136, 126, 135, 129, 138, 128, 137, 130, 152, 144, 132, 151, 143, 131, 154, 153,
-    133, 156, 172, 146, 163, 164, 243, 145, 155, 167, 148, 141, 168, 166, 165, 147, 196, 171, 170, 139, 140, 158, 198, 150,
-    244, 149, 142, 179, 183, 180, 169, 157, 181, 182, 159, 160, 189, 191, 184, 185, 174, 162, 161, 190, 175, 176, 194, 218,
-    215, 178, 177, 195, 173, 188, 217, 200, 234, 216, 193, 231, 192, 219, 199, 201, 223, 187, 203, 208, 233, 197, 186, 202,
-    245, 209, 210, 227, 207, 204, 235, 205, 206, 211, 251, 226, 224, 254, 222, 232, 220, 213, 259, 238, 228, 221, 225, 253,
-    212, 255, 236, 237, 239, 252, 229, 258, 230, 261, 240, 246, 247, 257, 260, 248, 249, 250, 256, 241, 262, 214, 263, 267,
-    242, 265, 269, 264, 268, 266, 270, 271, 272, 273, 274, 275, 276, 277, 278,
+    12, 15, 14, 13, 137, 0, 1, 2, 3, 4, 28, 30, 29, 20, 5, 31, 6, 7, 8, 40, 23, 9, 41, 32,
+    22, 39, 19, 21, 16, 24, 18, 46, 10, 35, 42, 27, 17, 11, 26, 45, 47, 25, 55, 59, 43, 57, 56, 72,
+    58, 60, 63, 51, 33, 44, 70, 34, 62, 48, 64, 68, 50, 37, 49, 36, 38, 65, 92, 53, 52, 54, 90, 91,
+    93, 108, 76, 96, 74, 101, 106, 107, 66, 112, 69, 100, 71, 77, 97, 80, 61, 75, 73, 67, 83, 95, 82, 79,
+    81, 78, 84, 85, 86, 120, 111, 117, 98, 109, 118, 102, 88, 128, 99, 119, 87, 124, 126, 105, 104, 94, 110, 103,
+    121, 125, 113, 123, 127, 116, 122, 89, 115, 114, 129, 138, 133, 132, 141, 131, 140, 130, 139, 157, 154, 136, 135, 156,
+    146, 155, 149, 165, 148, 158, 168, 147, 166, 161, 143, 173, 134, 243, 177, 171, 150, 160, 144, 170, 199, 167, 152, 169,
+    153, 176, 142, 145, 151, 181, 184, 185, 182, 183, 190, 193, 172, 186, 189, 163, 191, 164, 159, 188, 179, 162, 200, 180,
+    174, 204, 175, 192, 218, 178, 217, 234, 219, 203, 196, 198, 195, 233, 221, 206, 207, 216, 222, 187, 244, 197, 210, 227,
+    225, 232, 194, 238, 201, 202, 205, 208, 211, 209, 212, 254, 214, 237, 253, 224, 251, 220, 226, 230, 252, 236, 235, 213,
+    258, 229, 231, 261, 223, 228, 257, 259, 255, 245, 262, 240, 256, 241, 215, 260, 239, 242, 246, 247, 248, 249, 250, 266,
+    263, 265, 267, 270, 269, 264, 268, 271, 272, 273, 274, 275, 276, 277, 278,
 )
 
 
@@ -41,10 +41,6 @@
     bits = count.bit_length() - 1
     assert count == 1 << bits
     return bits
-
-
-def lowest(q, bits):
-    return bits if q == 0 else (q & -q).bit_length() - 1
 
 
 def position(relative, order):
@@ -72,7 +68,7 @@
         return (q + c) % 2
 
     def paired(self, q, c):
-        return q < 2
+        return q < 2 or c == 0
 
     def order(self, q, c):
         line = self.lines[self.side(q, c)]
@@ -81,8 +77,14 @@
     def last(self, q, c):
         return self.lines[self.side(q, c)][-1]
 
-    def children(self, q):
-        return [q | (1 << b) for b in range(lowest(q, self.nbits) - 1, -1, -1)]
+    def straight(self, c):
+        return False
+
+    def parent(self, q, c):
+        return 0 if self.straight(c) else q & (q - 1)
+
+    def children(self, q, c):
+        return [other for other in range(self.narrow - 1, 0, -1) if self.parent(other, c) == q]
 
 
 def steps_of(routes):
@@ -161,17 +163,28 @@
     return high, low
 
 
+def split_dot(a, b):
+    a_high, a_low = split(a)
+    b_high, b_low = split(b)
+    left = jnp.concatenate([a_high, a_low], axis=1)
+    right = jnp.concatenate(
+        [jnp.concatenate([b_high, b_low], axis=1), jnp.concatenate([b_high, jnp.zeros_like(b_low)], axis=1)], axis=0
+    )
+    both = jnp.dot(left, right, preferred_element_type=jnp.float32)
+    return both[:, : b.shape[1]] + both[:, b.shape[1]:]
+
+
 def tree_sum(values):
     while len(values) > 1:
         values = [a + b for a, b in zip(values[::2], values[1::2])]
     return values[0]
 
 
-def kernel(routes, sequence, slots, row_columns, tile_hbm, start, out, stage, tile_hi, tile_lo, turn_hi, turn_lo,
+def kernel(routes, sequence, slots, row_columns, tile_hbm, start_hbm, out, start, stage, tile_hi, tile_lo, turn_hi, turn_lo,
            rows_right, columns_right, trans, direct, whole_in, half_in, mate_rows, picks, picked, choices, chosen,
            whole_put, half_put, whole_back, half_back, passed, passed_mate, part, part_in, product, want, wants,
            grams, gram_in, gram_sum, gram_near, gram_part, gram_all, ns, roots,
-           stage_sem, send_sem, recv_sem, fence_sem):
+           stage_sem, start_sem, send_sem, recv_sem, fence_sem):
     wide, narrow, cuts = routes.wide, routes.narrow, routes.cuts
     me_w = lax.axis_index("wide")
     me_z = lax.axis_index("narrow")
@@ -206,6 +219,8 @@
             stage_sem.at[chunk % stages],
         )
 
+    begin = pltpu.make_async_copy(start_hbm, start, start_sem)
+    begin.start()
     for chunk in range(stages):
         fetch(chunk).start()
 
@@ -231,12 +246,13 @@
     def received(name):
         sent[name].wait_recv()
 
-    def all_gone():
+    def all_gone(*spared):
         for name, copy in sent.items():
-            if name not in waited:
+            if name not in waited and name[0] not in spared:
                 copy.wait_send()
                 waited.add(name)
 
+    begin.wait()
     for side in range(2):
         send(("want", side), want, wants.at[side], wide_peer(1 << routes.lines[side][-1]))
     wants_here = set()
@@ -333,7 +349,7 @@
             received(("rows", it, q, c))
         elif it == 0:
             ref[...] = start[pl.ds(c * n, n), :]
-        for child in routes.children(q):
+        for child in routes.children(q, c):
             send(("rows", it, child, c), ref, row_ref(it, child, c), near_peer(child ^ q))
         if not (routes.paired(q, c) and q % 2 == 1):
             start_step(it, q, c, 0)
@@ -424,19 +440,19 @@
         if not (routes.paired(q, c) and q % 2 == 1):
             received(("back", it, q, c, 0))
             value = value + (put_ref(it, q, c)[0] + back_ref(it, q, c)[1])
-        for child in routes.children(q):
+        for child in routes.children(q, c):
             received(("part", it, child, c))
             value = value + part_in[here(it), child - 1, c]
         if q > 0:
-            bit = 1 << lowest(q, routes.nbits)
             part[here(it), q - 1, c] = value
-            send(("part", it, q, c), part.at[here(it), q - 1, c], part_in.at[here(it), q - 1, c], near_peer(bit))
+            send(("part", it, q, c), part.at[here(it), q - 1, c], part_in.at[here(it), q - 1, c],
+                 near_peer(q ^ routes.parent(q, c)))
         elif it < ITERS - 1:
             product[pl.ds(c * n, n), :] = value
             if slots == ITERS:
                 row_ref(it + 1, 0, c)[...] = value
         else:
-            product[pl.ds(c * n, n), :] = jnp.dot(value, roots[it - 1], precision=HIGHEST)
+            product[pl.ds(c * n, n), :] = split_dot(value, roots[it - 1])
 
     grams_begun = set()
 
@@ -457,6 +473,8 @@
             send(("spread", it, mask), grams.at[it, slice_of(mask)], gram_in.at[it, mask], wide_peer(mask))
 
     def do_sum(it):
+        if it == ITERS - 1:
+            all_gone("spread")
         values = [grams[it, slice_of(0), :]]
         for mask in range(1, wide):
             received(("spread", it, mask))
@@ -466,6 +484,8 @@
             send(("near", it, mask), gram_sum.at[it], gram_near.at[it, mask], near_peer(mask))
 
     def do_all(it):
+        if it == ITERS - 1:
+            all_gone("near")
         values = [gram_sum[it]]
         for mask in range(1, narrow):
             received(("near", it, mask))
@@ -482,6 +502,8 @@
 
     def do_root(it, repeat):
         if repeat == 0:
+            if it == ITERS - 1:
+                all_gone("all")
             for mask in range(1, wide):
                 received(("all", it, mask))
             gram = gram_all[it]
@@ -493,10 +515,10 @@
             ns[2] = jnp.broadcast_to(jnp.sqrt(total_rows / scale), (width, width))
         else:
             current, inverse = ns[0], ns[1]
-            middle = 1.5 * identity() - 0.5 * jnp.dot(inverse, current, precision=HIGHEST)
-            inverse = jnp.dot(middle, inverse, precision=HIGHEST)
+            middle = 1.5 * identity() - 0.5 * split_dot(inverse, current)
+            inverse = split_dot(middle, inverse)
         if repeat < NS_STEPS - 1:
-            ns[0] = jnp.dot(current, middle, precision=HIGHEST)
+            ns[0] = split_dot(current, middle)
             ns[1] = inverse
         else:
             roots[it] = inverse * ns[2]
@@ -509,8 +531,8 @@
     actions["pass"] = do_pass
     for name in sequence:
         actions[name[0]](*name[1:])
-    out[...] = jnp.dot(product[...], roots[ITERS - 1], precision=HIGHEST)
     all_gone()
+    out[...] = split_dot(product[...], roots[ITERS - 1])
 
 
 def on_device(hamiltonian_tiles, row_columns, start_vectors):
@@ -540,10 +562,11 @@
         in_specs=[
             pl.BlockSpec(memory_space=pltpu.SMEM),
             pl.BlockSpec(memory_space=pl.ANY),
-            pl.BlockSpec(memory_space=pltpu.VMEM),
+            pl.BlockSpec(memory_space=pl.ANY),
         ],
         out_specs=pl.BlockSpec(memory_space=pltpu.VMEM),
         scratch_shapes=[
+            vmem(rows, width),
             vmem(2, stage_rows, order),
             vmem(order, order, dtype=bf16),
             vmem(order, order, dtype=bf16),
@@ -580,6 +603,7 @@
             vmem(3, width, width),
             vmem(ITERS, width, width),
             pltpu.SemaphoreType.DMA((2,)),
+            pltpu.SemaphoreType.DMA,
             pltpu.SemaphoreType.DMA((copies,)),
             pltpu.SemaphoreType.DMA((copies,)),
             pltpu.SemaphoreType.REGULAR,

time: 106 us -> 102 us (0.962)
  Pallas kernels: 105 us -> 100 us
    pallas_call x1, Pallas kernels: 105 us -> 100 us  [on_device(): pl.pallas_call(functools.partial(kernel, routes, sequence, slots), out_sh...]
where the time goes in v4:
time: 102 us
  Pallas kernels  100 us (98%)
  local copies, waits for them, and re-layouts  1.62 us (2%)
    pallas_call x1, Pallas kernels, on_device(): pl.pallas_call(functools.partial(kernel, routes, sequence, slots), out_sh...  100 us

profile of v4, /device:TPU:0, one launch (start us, length us, event | category | flops | bytes accessed | tf_op | source)
XLA Modules:
  0.0 102.1 jit_solution(984015059489742419)
XLA Ops:
  0.0 100.5 %shard_map.37 = f32[384,128]{1,0:T(8,128)} custom-call(s32[1,4]{1,0:T(1,128)} %row_columns.1, f32[1536,1536]{1,0:T(8,128)} %tile_hbm.1, f32[384,128]{1,0:T(8,128)} %start_hbm.1), custom_call_target="tpu_custom_call" | custom-call | tf_op jit(solution)/shard_map/pallas_call | solution.py:559
  100.5 1.6 %copy.5 = f32[384,128]{1,0:T(8,128)} copy(f32[384,128]{1,0:T(8,128)} %shard_map.37) | data formatting | bytes 393216

commit v5 on v4

--- a/solution.py
+++ b/solution.py
@@ -13,18 +13,18 @@
 MESH = pl.DeviceIdType.MESH
 LOAD_CHUNKS = 12
 ORDER = (
-    12, 15, 14, 13, 137, 0, 1, 2, 3, 4, 28, 30, 29, 20, 5, 31, 6, 7, 8, 40, 23, 9, 41, 32,
-    22, 39, 19, 21, 16, 24, 18, 46, 10, 35, 42, 27, 17, 11, 26, 45, 47, 25, 55, 59, 43, 57, 56, 72,
-    58, 60, 63, 51, 33, 44, 70, 34, 62, 48, 64, 68, 50, 37, 49, 36, 38, 65, 92, 53, 52, 54, 90, 91,
-    93, 108, 76, 96, 74, 101, 106, 107, 66, 112, 69, 100, 71, 77, 97, 80, 61, 75, 73, 67, 83, 95, 82, 79,
-    81, 78, 84, 85, 86, 120, 111, 117, 98, 109, 118, 102, 88, 128, 99, 119, 87, 124, 126, 105, 104, 94, 110, 103,
-    121, 125, 113, 123, 127, 116, 122, 89, 115, 114, 129, 138, 133, 132, 141, 131, 140, 130, 139, 157, 154, 136, 135, 156,
-    146, 155, 149, 165, 148, 158, 168, 147, 166, 161, 143, 173, 134, 243, 177, 171, 150, 160, 144, 170, 199, 167, 152, 169,
-    153, 176, 142, 145, 151, 181, 184, 185, 182, 183, 190, 193, 172, 186, 189, 163, 191, 164, 159, 188, 179, 162, 200, 180,
-    174, 204, 175, 192, 218, 178, 217, 234, 219, 203, 196, 198, 195, 233, 221, 206, 207, 216, 222, 187, 244, 197, 210, 227,
-    225, 232, 194, 238, 201, 202, 205, 208, 211, 209, 212, 254, 214, 237, 253, 224, 251, 220, 226, 230, 252, 236, 235, 213,
-    258, 229, 231, 261, 223, 228, 257, 259, 255, 245, 262, 240, 256, 241, 215, 260, 239, 242, 246, 247, 248, 249, 250, 266,
-    263, 265, 267, 270, 269, 264, 268, 271, 272, 273, 274, 275, 276, 277, 278,
+    13, 14, 0, 1, 2, 15, 3, 12, 4, 30, 29, 21, 31, 5, 6, 7, 22, 8, 9, 23, 10, 28, 40, 42,
+    20, 33, 72, 44, 16, 11, 41, 18, 35, 19, 25, 17, 34, 54, 26, 48, 27, 45, 39, 50, 32, 24, 55, 58,
+    59, 74, 57, 47, 46, 56, 49, 38, 37, 76, 60, 64, 65, 69, 80, 36, 53, 82, 43, 73, 86, 93, 67, 92,
+    52, 51, 78, 108, 91, 68, 62, 97, 77, 66, 61, 107, 79, 70, 101, 85, 106, 81, 75, 71, 84, 83, 87, 120,
+    112, 95, 99, 63, 105, 119, 88, 98, 118, 117, 94, 103, 110, 89, 100, 124, 109, 137, 102, 96, 125, 126, 122, 116,
+    104, 111, 128, 121, 113, 114, 127, 123, 90, 132, 141, 115, 130, 139, 134, 129, 138, 157, 131, 140, 135, 133, 155, 149,
+    154, 147, 168, 136, 161, 156, 146, 148, 180, 166, 176, 144, 243, 165, 170, 172, 145, 159, 142, 143, 158, 198, 167, 151,
+    153, 200, 150, 160, 174, 169, 152, 181, 182, 183, 184, 191, 193, 173, 186, 190, 162, 194, 202, 163, 171, 204, 175, 197,
+    164, 208, 177, 178, 217, 179, 185, 187, 192, 218, 196, 225, 201, 219, 223, 212, 232, 188, 189, 205, 244, 233, 199, 229,
+    209, 207, 226, 195, 210, 203, 234, 206, 211, 213, 254, 238, 215, 262, 230, 220, 251, 235, 252, 221, 227, 214, 245, 258,
+    236, 222, 231, 224, 253, 237, 228, 255, 261, 256, 241, 260, 246, 242, 216, 257, 240, 239, 247, 259, 248, 249, 250, 266,
+    270, 264, 268, 265, 269, 263, 267, 271, 272, 273, 274, 275, 276, 277, 278,
 )
 
 
@@ -54,25 +54,20 @@
         self.cuts = max(1, 4 * 4 // narrow)
         upper = list(range(1, self.wbits))
         self.lines = [upper, upper[::-1]]
-        self.whole = []
-        self.half = []
-        for q in range(narrow):
-            for c in range(self.cuts):
-                if self.paired(q, c):
-                    if q % 2 == 0:
-                        self.whole.append((q, c))
-                else:
-                    self.half.append((q, c))
+        pieces = [(q, c) for q in range(narrow) for c in range(self.cuts)]
+        self.whole = [(q, c) for q, c in pieces if q == 0]
+        self.given = [(q, c) for q, c in pieces if self.served(q, c)]
+        self.half = [(q, c) for q, c in pieces if q > 0 and not self.served(q, c)]
 
     def side(self, q, c):
         return (q + c) % 2
 
-    def paired(self, q, c):
-        return q < 2 or c == 0
+    def served(self, q, c):
+        return q > 0 and (q == 1 or (q == 3 and c == 3))
 
     def order(self, q, c):
         line = self.lines[self.side(q, c)]
-        return line + [0] if self.paired(q, c) else line[:-1] + [0]
+        return line + [0] if q == 0 else line[:-1] + [0]
 
     def last(self, q, c):
         return self.lines[self.side(q, c)][-1]
@@ -99,19 +94,16 @@
         for level in range(1, routes.wbits):
             for q in quarters:
                 for c in cuts:
-                    paired = routes.paired(q, c)
-                    if paired and q % 2 == 1:
-                        continue
-                    if level < len(routes.order(q, c)):
+                    if not routes.served(q, c) and level < len(routes.order(q, c)):
                         steps.append(("step", it, q, c, level))
         for q in quarters:
             for c in cuts:
-                if not (routes.paired(q, c) and q % 2 == 1):
+                if q > 0:
                     steps.append(("pick", it, q, c))
         for q in quarters[::-1]:
             steps.append(("trans", it, q))
             for c in cuts:
-                if not (routes.paired(q, c) and q % 2 == 0):
+                if q > 0:
                     steps.append(("pass", it, q, c))
         for q in quarters:
             for c in cuts:
@@ -120,14 +112,12 @@
             steps.append(("direct", it, q))
         for q in quarters[::-1]:
             for c in cuts:
-                if not (routes.paired(q, c) and q % 2 == 1):
+                if not routes.served(q, c):
                     steps.append(("put", it, q, c))
         for level in range(routes.wbits - 1, 0, -1):
             for q in quarters[::-1]:
                 for c in cuts:
-                    if routes.paired(q, c) and q % 2 == 1:
-                        continue
-                    if level < len(routes.order(q, c)):
+                    if not routes.served(q, c) and level < len(routes.order(q, c)):
                         steps.append(("down", it, q, c, level))
         if it > 0:
             steps.append(("spread", it - 1))
@@ -151,7 +141,7 @@
     pieces = routes.narrow * routes.cuts
     for it in range(ITERS):
         count += 2 * (routes.narrow - 1) * routes.cuts
-        count += 2 * len(routes.whole) * (routes.wbits + 1)
+        count += 2 * len(routes.whole) * routes.wbits + 2 * len(routes.given)
         count += 2 * len(routes.half) * routes.wbits
         count += 2 * (routes.wide - 1) + routes.narrow - 1
     return count
@@ -197,6 +187,7 @@
     total_rows = float(wide * order)
     whole_at = {unit: place for place, unit in enumerate(routes.whole)}
     half_at = {unit: place for place, unit in enumerate(routes.half)}
+    given_at = {unit: place for place, unit in enumerate(routes.given)}
 
     def wide_peer(mask):
         return {"wide": flip(me_w, mask), "narrow": me_z}
@@ -224,9 +215,8 @@
     for chunk in range(stages):
         fetch(chunk).start()
 
-    mate = flip(me_z, 1)
-    own_want = row_columns[0, me_z] ^ me_w
-    mate_want = row_columns[0, mate] ^ me_w
+    near_wants = [row_columns[0, flip(me_z, q)] ^ me_w for q in range(narrow)]
+    own_want = near_wants[0]
     want[...] = jnp.full(want.shape, own_want, jnp.int32)
     pl.semaphore_wait(barrier, len(peers))
 
@@ -267,22 +257,22 @@
         return it % slots
 
     def gathered(it, q, c):
-        if routes.paired(q, c):
+        if q == 0:
             return whole_in.at[here(it), whole_at[q, c]]
         return half_in.at[here(it), half_at[q, c]]
 
     def row_ref(it, q, c):
-        if routes.paired(q, c) and q % 2 == 1:
-            return mate_rows.at[here(it), whole_at[q - 1, c]]
+        if routes.served(q, c):
+            return mate_rows.at[here(it), given_at[q, c]]
         return gathered(it, q, c).at[0]
 
     def put_ref(it, q, c):
-        if routes.paired(q, c):
+        if q == 0:
             return whole_put.at[here(it), whole_at[q, c]]
         return half_put.at[here(it), half_at[q, c]]
 
     def back_ref(it, q, c):
-        if routes.paired(q, c):
+        if q == 0:
             return whole_back.at[here(it), whole_at[q, c]]
         return half_back.at[here(it), half_at[q, c]]
 
@@ -351,7 +341,7 @@
             ref[...] = start[pl.ds(c * n, n), :]
         for child in routes.children(q, c):
             send(("rows", it, child, c), ref, row_ref(it, child, c), near_peer(child ^ q))
-        if not (routes.paired(q, c) and q % 2 == 1):
+        if not routes.served(q, c):
             start_step(it, q, c, 0)
         keep_split(rows_right, piece_at(q, c), ref[...])
 
@@ -359,14 +349,21 @@
         received(("gather", it, q, c, level - 1))
         start_step(it, q, c, level)
 
+    complete = set()
+
+    def finish_gather(it, q, c):
+        if (it, q, c) not in complete:
+            complete.add((it, q, c))
+            received(("gather", it, q, c, len(routes.order(q, c)) - 1))
+
     def do_pick(it, q, c):
-        levels = len(routes.order(q, c))
-        received(("gather", it, q, c, levels - 1))
-        if routes.paired(q, c):
-            at = whole_at[q, c]
-            picks[here(it), at] = choose(gathered(it, q, c), wide, position(mate_want, routes.order(q, c)))
-            send(("pick", it, q, c), picks.at[here(it), at], picked.at[here(it), at], near_peer(1))
-        else:
+        if routes.served(q, c):
+            finish_gather(it, 0, c)
+            at = given_at[q, c]
+            picks[here(it), at] = choose(gathered(it, 0, c), wide, position(near_wants[q], routes.order(0, c)))
+            send(("pick", it, q, c), picks.at[here(it), at], picked.at[here(it), at], near_peer(q))
+        else:
+            finish_gather(it, q, c)
             at = half_at[q, c]
             choices[here(it), at] = choose(gathered(it, q, c), wide // 2, far_codes(q, c))
             send(
@@ -375,13 +372,14 @@
             )
 
     def do_column(it, q, c):
-        if routes.paired(q, c):
-            if q % 2 == 0:
-                value = choose(gathered(it, q, c), wide, position(own_want, routes.order(q, c)))
-            else:
-                received(("pick", it, q - 1, c))
-                value = picked[here(it), whole_at[q - 1, c]]
-        else:
+        if q == 0:
+            finish_gather(it, q, c)
+            value = choose(gathered(it, q, c), wide, position(own_want, routes.order(q, c)))
+        elif routes.served(q, c):
+            received(("pick", it, q, c))
+            value = picked[here(it), given_at[q, c]]
+        else:
+            finish_gather(it, q, c)
             received(("pick", it, q, c))
             value = choose(gathered(it, q, c), wide // 2, position(own_want, routes.order(q, c)))
             value = jnp.where((own_want >> routes.last(q, c)) & 1 == 1, chosen[here(it), half_at[q, c]], value)
@@ -402,8 +400,8 @@
 
     def do_pass(it, q, c):
         source = trans.at[here(it), piece_at(q, c)]
-        if routes.paired(q, c):
-            send(("pass", it, q, c), source, passed_mate.at[here(it), whole_at[q - 1, c]], near_peer(1))
+        if routes.served(q, c):
+            send(("pass", it, q, c), source, passed_mate.at[here(it), given_at[q, c]], near_peer(q))
         else:
             send(
                 ("pass", it, q, c), source, passed.at[here(it), half_at[q, c]],
@@ -414,17 +412,23 @@
         mine = trans[here(it), piece_at(q, c), :]
         ref = put_ref(it, q, c)
         places = routes.order(q, c)
-        if routes.paired(q, c):
-            received(("pass", it, q + 1, c))
-            other = passed_mate[here(it), whole_at[q, c]]
-            count, first, second = wide, position(own_want, places), position(mate_want, places)
+        if q == 0:
+            count, first = wide, position(own_want, places)
+            others = []
+            for near in range(1, narrow):
+                if routes.served(near, c):
+                    received(("pass", it, near, c))
+                    others.append((position(near_wants[near], places), passed_mate[here(it), given_at[near, c]]))
         else:
             received(("pass", it, q, c))
-            other = passed[here(it), half_at[q, c]]
-            count, second = wide // 2, far_codes(q, c)
+            count = wide // 2
+            others = [(far_codes(q, c), passed[here(it), half_at[q, c]])]
             first = position(own_want, places) + wide * ((own_want >> routes.last(q, c)) & 1)
         for p in range(count):
-            ref[p] = jnp.where(first == p, mine, 0.0) + jnp.where(second == p, other, 0.0)
+            value = jnp.where(first == p, mine, 0.0)
+            for place, other in others:
+                value = value + jnp.where(place == p, other, 0.0)
+            ref[p] = value
         start_back(it, q, c, len(places) - 1)
 
     def do_down(it, q, c, level):
@@ -437,7 +441,7 @@
 
     def do_merge(it, q, c):
         value = direct[piece_at(q, c), :]
-        if not (routes.paired(q, c) and q % 2 == 1):
+        if not routes.served(q, c):
             received(("back", it, q, c, 0))
             value = value + (put_ref(it, q, c)[0] + back_ref(it, q, c)[1])
         for child in routes.children(q, c):
@@ -548,7 +552,7 @@
     if len(ORDER) == len(sequence):
         sequence = [sequence[place] for place in ORDER]
     copies = sends_of(routes)
-    wholes, halves = max(1, len(routes.whole)), max(1, len(routes.half))
+    wholes, halves, givens = len(routes.whole), max(1, len(routes.half)), max(1, len(routes.given))
     f32, bf16 = jnp.float32, jnp.bfloat16
     stage_rows = order // LOAD_CHUNKS
     slice_rows = width // wide
@@ -578,9 +582,9 @@
             vmem(order, width),
             vmem(slots, wholes, wide, n, width),
             vmem(slots, halves, wide // 2, n, width),
-            vmem(slots, wholes, n, width),
-            vmem(slots, wholes, n, width),
-            vmem(slots, wholes, n, width),
+            vmem(slots, givens, n, width),
+            vmem(slots, givens, n, width),
+            vmem(slots, givens, n, width),
             vmem(slots, halves, n, width),
             vmem(slots, halves, n, width),
             vmem(slots, wholes, wide, n, width),
@@ -588,7 +592,7 @@
             vmem(slots, wholes, wide, n, width),
             vmem(slots, halves, wide // 2, n, width),
             vmem(slots, halves, n, width),
-            vmem(slots, wholes, n, width),
+            vmem(slots, givens, n, width),
             vmem(slots, narrow - 1, cuts, n, width),
             vmem(slots, narrow - 1, cuts, n, width),
             vmem(rows, width),

time: 102 us -> 102 us (level)
  no operation moved by 1% of the time
where the time goes in v5:
time: 102 us
  Pallas kernels  100 us (98%)
  local copies, waits for them, and re-layouts  1.62 us (2%)
    pallas_call x1, Pallas kernels, on_device(): pl.pallas_call(functools.partial(kernel, routes, sequence, slots), out_sh...  100 us

profile of v5, /device:TPU:0, one launch (start us, length us, event | category | flops | bytes accessed | tf_op | source)
XLA Modules:
  0.0 101.6 jit_solution(2043236396431263144)
XLA Ops:
  0.0 100.0 %shard_map.37 = f32[384,128]{1,0:T(8,128)} custom-call(s32[1,4]{1,0:T(1,128)} %row_columns.1, f32[1536,1536]{1,0:T(8,128)} %tile_hbm.1, f32[384,128]{1,0:T(8,128)} %start_hbm.1), custom_call_target="tpu_custom_call" | custom-call | tf_op jit(solution)/shard_map/pallas_call | solution.py:563
  100.0 1.6 %copy.5 = f32[384,128]{1,0:T(8,128)} copy(f32[384,128]{1,0:T(8,128)} %shard_map.37) | data formatting | bytes 393216
